TPU v7x, 256 devices: a whole 4x4x8 slice. The times are simulated.
256 devices in a mesh: gx: 16 (over z_lo, y, core), gy: 16 (over z_hi, x).
Axes of the slice: x: 4, y: 4, z: 8 (z_hi: 4, z_lo: 2; z = z_hi * 2 + z_lo), core: 2. Of those that a mesh axis runs over, the one named last changes fastest.
Arguments:
- state: float32 [286, 2, 32, 2048], P(None, None, 'gy', 'gx'), may hold values from -6 to 6
- adjoint: float32 [286, 2, 32, 2048], P(None, None, 'gy', 'gx'), may hold values from -6 to 6
- upwind_pos: float32 [3, 286, 286], replicated, may hold values from -0.375 to 0.375
- upwind_neg: float32 [3, 286, 286], replicated, may hold values from -0.375 to 0.375
- collision: float32 [35, 35, 35], replicated, may hold values from -0.15625 to 0.15625
- relax: float32 [286], replicated, may hold values from 0.1 to 2
- wall_table: float32 [3, 286], replicated, may hold values from 0 to 2
- drag_weights: float32 [286], replicated, may hold values from -6 to 6
- block_inverse: float32 [286, 286], replicated, may hold values from -0.375 to 0.375
- cell_codes: int32 [2, 32, 2048], P(None, 'gy', 'gx'), may hold values from 0 to 3
- wall_mask: int32 [2, 32, 2048], P(None, 'gy', 'gx'), may hold values 0 or 1
Outputs:
- state_next: float32 [286, 2, 32, 2048], P(None, None, 'gy', 'gx')
- adjoint_next: float32 [286, 2, 32, 2048], P(None, None, 'gy', 'gx')
All inputs are finite; a program needn't handle non-finite values. No bound on the sum of `wall_mask` on one device may be relied on, other than what follows from the above.
Results may differ from a plain program's by a relative error of at most 0.0003.
Values sent between devices are 32-bit elements; how exact they have to be, the bound alone decides.
No kernel may reach another device: no remote copies, remote signals or barrier semaphores. Data moves between devices by JAX's collectives and lax.ppermute only.
A program may use at most 64 MiB of HBM per device.

v0:
```python
import jax
import jax.numpy as jnp
from jax import lax
from jax.sharding import PartitionSpec as P


def from_behind(block, axis, distance):
    devices = range(lax.axis_size(axis))
    route = [(i - distance, i) for i in devices if i - distance in devices]
    return lax.ppermute(block, axis, route)


def apply_matrix(matrix, field):
    return jnp.einsum("ab,bpyx->apyx", matrix, field, precision=lax.Precision.HIGHEST)


def apply_transposed(matrix, field):
    return jnp.einsum("ba,bpyx->apyx", matrix, field, precision=lax.Precision.HIGHEST)


def neighbours(center, received):
    x_prev, x_next, y_prev, y_next = received
    lanes = lax.broadcasted_iota(jnp.int32, center.shape, 3)
    rows = lax.broadcasted_iota(jnp.int32, center.shape, 2)
    last_lane = center.shape[3] - 1
    last_row = center.shape[2] - 1
    xminus = jnp.where(lanes == 0, x_prev, jnp.roll(center, 1, axis=3))
    xplus = jnp.where(lanes == last_lane, x_next, jnp.roll(center, -1, axis=3))
    yminus = jnp.where(rows == 0, y_prev, jnp.roll(center, 1, axis=2))
    yplus = jnp.where(rows == last_row, y_next, jnp.roll(center, -1, axis=2))
    zminus = jnp.roll(center, 1, axis=1)
    zplus = jnp.roll(center, -1, axis=1)
    return ((xminus, yminus, zminus), (xplus, yplus, zplus))


def on_device(
    state,
    adjoint,
    upwind_pos,
    upwind_neg,
    collision,
    relax,
    wall_table,
    drag_weights,
    block_inverse,
    cell_codes,
    wall_mask,
):
    state_recv = (
        from_behind(state[:, :, :, -1:], "gx", 1),
        from_behind(state[:, :, :, :1], "gx", -1),
        from_behind(state[:, :, -1:, :], "gy", 1),
        from_behind(state[:, :, :1, :], "gy", -1),
    )
    adjoint_recv = (
        from_behind(adjoint[:, :, :, -1:], "gx", 1),
        from_behind(adjoint[:, :, :, :1], "gx", -1),
        from_behind(adjoint[:, :, -1:, :], "gy", 1),
        from_behind(adjoint[:, :, :1, :], "gy", -1),
    )
    lowest = collision.shape[0]
    minus_all, plus_all = neighbours(state, state_recv)
    stream = jnp.zeros_like(state)
    for direction in range(3):
        stream = stream + apply_matrix(upwind_pos[direction], state - minus_all[direction])
        stream = stream + apply_matrix(upwind_neg[direction], plus_all[direction] - state)
    adminus, adplus = neighbours(adjoint, adjoint_recv)
    adstream = jnp.zeros_like(adjoint)
    for direction in range(3):
        adstream = adstream + apply_transposed(upwind_pos[direction], adjoint - adplus[direction])
        adstream = adstream + apply_transposed(upwind_neg[direction], adminus[direction] - adjoint)
    onehot = (cell_codes[None] == jnp.arange(1, 4, dtype=jnp.int32)[:, None, None, None]).astype(
        jnp.float32
    )
    damp = relax[:, None, None, None] + jnp.einsum(
        "cm,cpyx->mpyx", wall_table, onehot, precision=lax.Precision.HIGHEST
    )
    walls = wall_mask.astype(jnp.float32)[None]
    state_low = state[:lowest]
    adjoint_low = adjoint[:lowest]
    products = state_low[:, None] * state_low[None, :]
    gain = jnp.einsum("kab,abpyx->kpyx", collision, products, precision=lax.Precision.HIGHEST)
    symmetric = collision + jnp.transpose(collision, (0, 2, 1))
    cross = adjoint_low[:, None] * state_low[None, :]
    adgain = jnp.einsum("kij,kjpyx->ipyx", symmetric, cross, precision=lax.Precision.HIGHEST)
    primal_res = stream.at[:lowest].add(-gain) + damp * state
    state_next = state - 0.5 * apply_matrix(block_inverse, primal_res)
    adjoint_res = (
        adstream.at[:lowest].add(-adgain)
        + damp * adjoint
        - walls * drag_weights[:, None, None, None]
    )
    adjoint_next = adjoint - 0.5 * apply_transposed(block_inverse, adjoint_res)
    return (state_next, adjoint_next)


def solution(mesh):
    in_specs = (
        P(None, None, "gy", "gx"),
        P(None, None, "gy", "gx"),
        P(),
        P(),
        P(),
        P(),
        P(),
        P(),
        P(),
        P(None, "gy", "gx"),
        P(None, "gy", "gx"),
    )
    out_specs = (P(None, None, "gy", "gx"), P(None, None, "gy", "gx"))
    return jax.shard_map(
        on_device, mesh=mesh, in_specs=in_specs, out_specs=out_specs, check_vma=False
    )
```

profile of v0, /device:TPU:224, one launch (start us, length us, event | category | flops | bytes accessed | tf_op | source)
XLA Modules:
  0.0 96.9 jit_solution(3545710191324812922)
XLA Ops:
  0.6 0.0 copy-start
  0.6 0.0 copy-start.1
  0.7 2.1 %fusion.122 = (f32[286,2,2,1]{3,2,1,0:T(2,128)S(1)}, f32[286,2,2,1]{3,2,1,0:T(2,128)S(1)}) fusion(f32[286,2,2,128]{3,2,1,0:T(2,128)} %param.16), kind=kLoop, calls=%fused_computation.135 | loop fusion | bytes 18304 | tf_op jit(solution)/shard_map/slice | solution.py:56
  2.8 0.0 copy-start.2
  2.8 0.4 copy.149
  3.2 4.9 %collective-permute-start.4 = (f32[286,2,2,1]{0,2,3,1:T(2,128)S(1)}, f32[286,2,2,1]{0,2,3,1:T(2,128)S(1)}, u32[]{:S(2)}, u32[]{:S(2)}) collective-permute-start(f32[286,2,2,1]{0,2,3,1:T(2,128)S(1)} %copy.149), channel_id=1, source_target_pairs={{16,0},{32,16},{48,32},{64,48},{80,64},{96,80},{112,96},{128,112},... | collective-permute-start | bytes 13736 | tf_op jit(solution)/shard_map/ppermute | solution.py:10
  8.1 0.4 copy.150
  8.5 1.9 %collective-permute-start.5 = (f32[286,2,2,1]{0,2,3,1:T(2,128)S(1)}, f32[286,2,2,1]{0,2,3,1:T(2,128)S(1)}, u32[]{:S(2)}, u32[]{:S(2)}) collective-permute-start(f32[286,2,2,1]{0,2,3,1:T(2,128)S(1)} %copy.150), channel_id=1, source_target_pairs={{0,16},{16,32},{32,48},{48,64},{64,80},{80,96},{96,112},{112,128},... | collective-permute-start | bytes 13736 | tf_op jit(solution)/shard_map/ppermute | solution.py:10
  10.5 1.2 %fusion.121 = (f32[286,2,1,128]{3,2,1,0:T(1,128)}, f32[286,2,1,128]{3,2,1,0:T(1,128)S(1)}) fusion(f32[286,2,2,128]{3,2,1,0:T(2,128)S(1)} %copy-done.1), kind=kLoop, calls=%fused_computation.134 | loop fusion | bytes 1171456 | tf_op jit(solution)/shard_map/jit(_roll_static)/slice | solution.py:30
  11.7 5.6 %collective-permute-start.6 = (f32[286,2,1,128]{3,0,2,1:T(8,128)S(1)}, f32[286,2,1,128]{3,0,2,1:T(8,128)}, u32[]{:S(2)}, u32[]{:S(2)}) collective-permute-start(f32[286,2,1,128]{3,0,2,1:T(8,128)S(1)} %copy.195), channel_id=1, source_target_pairs={{1,0},{2,1},{3,2},{4,3},{5,4},{6,5},{7,6},{8,7},{9,8},{10,9},{11,1... | collective-permute-start | bytes 878600 | tf_op jit(solution)/shard_map/ppermute | solution.py:10
  17.2 0.8 fusion.127
  18.0 0.0 copy-start.9
  18.0 0.4 copy.147
  18.4 1.9 %collective-permute-start = (f32[286,2,2,1]{0,2,3,1:T(2,128)S(1)}, f32[286,2,2,1]{0,2,3,1:T(2,128)S(1)}, u32[]{:S(2)}, u32[]{:S(2)}) collective-permute-start(f32[286,2,2,1]{0,2,3,1:T(2,128)S(1)} %copy.147), channel_id=1, source_target_pairs={{0,16},{16,32},{32,48},{48,64},{64,80},{80,96},{96,112},{112,128},... | collective-permute-start | bytes 13736 | tf_op jit(solution)/shard_map/ppermute | solution.py:10
  20.4 0.4 copy.148
  20.7 5.8 %collective-permute-start.1 = (f32[286,2,2,1]{0,2,3,1:T(2,128)S(1)}, f32[286,2,2,1]{0,2,3,1:T(2,128)S(1)}, u32[]{:S(2)}, u32[]{:S(2)}) collective-permute-start(f32[286,2,2,1]{0,2,3,1:T(2,128)S(1)} %copy.148), channel_id=1, source_target_pairs={{16,0},{32,16},{48,32},{64,48},{80,64},{96,80},{112,96},{128,112},... | collective-permute-start | bytes 13736 | tf_op jit(solution)/shard_map/ppermute | solution.py:10
  26.5 1.8 %fusion.123 = (f32[286,2,2,127]{3,2,1,0:T(2,128)}, f32[286,2,2,127]{3,2,1,0:T(2,128)}) fusion(f32[286,2,2,128]{3,2,1,0:T(2,128)S(1)} %copy-done.1), kind=kLoop, calls=%fused_computation.136 | loop fusion | bytes 2324608 | tf_op jit(solution)/shard_map/jit(_roll_static)/slice | solution.py:27
  28.4 1.1 %fusion.120 = (f32[286,1,2,128]{3,2,1,0:T(2,128)}, f32[286,1,2,128]{3,2,1,0:T(2,128)}) fusion(f32[286,2,2,128]{3,2,1,0:T(2,128)S(1)} %copy-done.1), kind=kLoop, calls=%fused_computation.133 | loop fusion | bytes 1171456 | tf_op jit(solution)/shard_map/jit(_roll_static)/slice | solution.py:32
  29.4 1.8 %fusion.126 = (f32[286,2,2,127]{3,2,1,0:T(2,128)}, f32[286,2,2,127]{3,2,1,0:T(2,128)}) fusion(f32[286,2,2,128]{3,2,1,0:T(2,128)S(1)} %copy-done.2), kind=kLoop, calls=%fused_computation.139 | loop fusion | bytes 2324608 | tf_op jit(solution)/shard_map/jit(_roll_static)/slice | solution.py:28
  31.3 1.0 %fusion.124 = (f32[286,1,2,128]{3,2,1,0:T(2,128)}, f32[286,1,2,128]{3,2,1,0:T(2,128)}) fusion(f32[286,2,2,128]{3,2,1,0:T(2,128)S(1)} %copy-done.2), kind=kLoop, calls=%fused_computation.137 | loop fusion | bytes 1171456 | tf_op jit(solution)/shard_map/jit(_roll_static)/slice | solution.py:31
  32.3 1.3 %fusion.125 = (f32[286,2,1,128]{3,2,1,0:T(1,128)}, f32[286,2,1,128]{3,2,1,0:T(1,128)}) fusion(f32[286,2,2,128]{3,2,1,0:T(2,128)S(1)} %copy-done.2), kind=kLoop, calls=%fused_computation.138 | loop fusion | bytes 1171456 | tf_op jit(solution)/shard_map/slice | solution.py:52
  33.6 1.3 %fusion.14 = f32[286,2,2,128]{3,0,2,1:T(8,128)} fusion(f32[286]{0:T(512)S(1)} %copy-done.30, f32[3,286]{1,0:T(4,128)S(1)} %copy-done.29, s32[2,2,128]{2,1,0:T(2,128)S(1)} %copy-done.31, s32[3]{0:T(128)S(1)} %iota_add_fusion), kind=kOutput, calls=%fused_computation.27 | convolution fusion | flops 5419520 | bytes 592364 | tf_op jit(solution)/shard_map/cm,cpyx->mpyx/dot_general | solution.py:75
  34.9 0.7 copy.196
  35.7 1.2 %copy.112 = f32[35,35,35]{1,2,0:T(8,128)} copy(f32[35,35,35]{2,1,0:T(8,128)S(1)} %copy-done.13) | data formatting | bytes 343000 | tf_op args[4]
  36.9 1.7 %copy.194 = f32[286,2,1,128]{3,0,2,1:T(8,128)} copy(f32[286,2,1,128]{3,2,1,0:T(1,128)} %get-tuple-element.50) | data formatting | bytes 585728
  38.6 0.7 copy.193
  39.4 1.9 %collective-permute-start.7 = (f32[286,2,1,128]{3,0,2,1:T(8,128)}, f32[286,2,1,128]{3,0,2,1:T(8,128)}, u32[]{:S(2)}, u32[]{:S(2)}) collective-permute-start(f32[286,2,1,128]{3,0,2,1:T(8,128)} %copy.196), channel_id=1, source_target_pairs={{0,1},{1,2},{2,3},{3,4},{4,5},{5,6},{6,7},{7,8},{8,9},{9,10},{10,1... | collective-permute-start | bytes 878600 | tf_op jit(solution)/shard_map/ppermute | solution.py:10
  41.3 0.9 copy.93
  42.2 1.9 %collective-permute-start.2 = (f32[286,2,1,128]{3,0,2,1:T(8,128)}, f32[286,2,1,128]{3,0,2,1:T(8,128)}, u32[]{:S(2)}, u32[]{:S(2)}) collective-permute-start(f32[286,2,1,128]{3,0,2,1:T(8,128)} %copy.194), channel_id=1, source_target_pairs={{0,1},{1,2},{2,3},{3,4},{4,5},{5,6},{6,7},{7,8},{8,9},{9,10},{10,1... | collective-permute-start | bytes 878600 | tf_op jit(solution)/shard_map/ppermute | solution.py:10
  44.1 0.9 copy.98
  45.0 6.9 %collective-permute-start.3 = (f32[286,2,1,128]{3,0,2,1:T(8,128)}, f32[286,2,1,128]{3,0,2,1:T(8,128)}, u32[]{:S(2)}, u32[]{:S(2)}) collective-permute-start(f32[286,2,1,128]{3,0,2,1:T(8,128)} %copy.193), channel_id=1, source_target_pairs={{1,0},{2,1},{3,2},{4,3},{5,4},{6,5},{7,6},{8,7},{9,8},{10,9},{11,1... | collective-permute-start | bytes 878600 | tf_op jit(solution)/shard_map/ppermute | solution.py:10
  52.0 0.9 copy.74
  52.9 0.9 copy.78
  53.8 5.4 %fusion.102 = (f32[286,2,2,128]{3,2,1,0:T(2,128)S(1)}, f32[286,2,2,128]{3,2,1,0:T(2,128)S(1)}, f32[286,2,2,128]{3,2,1,0:T(2,128)S(1)}, f32[286,2,2,128]{3,2,1,0:T(2,128)S(1)}) fusion(f32[286,2,2,128]{3,2,1,0:T(2,128)S(1)} %copy-done.1, f32[286,1,2,128]{3,2,1,0:T(2,128)} %get-tuple-element.39, f32[286,1,2,128]{3,2,1,0:T(2,128)} %get-tuple-element.38, ...), kind=kLoop, calls=%fused_computation.110 | loop fusion | flops 1317888 | bytes 4695232 | tf_op jit(solution)/shard_map/sub | solution.py:71
  59.2 0.0 copy-start.5
  59.2 1.2 %fusion.41 = f32[2,2,128,286]{2,3,1,0:T(8,128)S(1)} fusion(f32[286,2,2,128]{3,2,1,0:T(2,128)S(1)} %get-tuple-element.37, f32[3,286,286]{2,1,0:T(8,128)S(1)} %copy-done.3), kind=kOutput, calls=%fused_computation.43 | convolution fusion | flops 502554624 | bytes 1613824 | tf_op jit(solution)/shard_map/ba,bpyx->apyx/dot_general | solution.py:18
  60.4 0.0 copy-start.10
  60.5 0.0 copy-start.21
  60.5 0.1 copy-done.5
  60.5 1.2 %convolution_add_fusion.4 = f32[2,2,128,286]{2,3,1,0:T(8,128)S(1)} fusion(f32[2,2,128,286]{2,3,1,0:T(8,128)S(1)} %fusion.41, f32[286,2,2,128]{3,2,1,0:T(2,128)S(1)} %get-tuple-element.36, f32[3,286,286]{2,1,0:T(8,128)S(1)} %copy-done.5), kind=kOutput, calls=%fused_computation.13 | convolution fusion | flops 502701056 | bytes 2203648 | tf_op jit(solution)/shard_map/ba,bpyx->apyx/dot_general | solution.py:18
  61.8 0.1 copy-done.21
  61.9 3.5 %fusion.104 = (f32[286,2,2,128]{3,2,1,0:T(2,128)}, f32[286,2,2,128]{3,2,1,0:T(2,128)}, f32[286,2,2,128]{3,2,1,0:T(2,128)S(1)}, f32[286,2,2,128]{3,2,1,0:T(2,128)S(1)}) fusion(f32[286,2,2,128]{3,2,1,0:T(2,128)S(1)} %copy-done.2, f32[286,1,2,128]{3,2,1,0:T(2,128)S(1)} %copy-done.24, f32[286,1,2,128]{3,2,1,0:T(2,128)S(1)} %copy-done.23, ...), kind=kLoop, calls=%fused_computation.112 | loop fusion | flops 1317888 | bytes 4695232 | tf_op jit(solution)/shard_map/sub | solution.py:66
  65.4 1.2 %fusion.46 = f32[2,2,128,286]{2,3,1,0:T(8,128)S(1)} fusion(f32[286,2,2,128]{3,2,1,0:T(2,128)S(1)} %get-tuple-element.47, f32[3,286,286]{2,1,0:T(8,128)S(1)} %copy-done.3), kind=kOutput, calls=%fused_computation.48 | convolution fusion | flops 502554624 | bytes 1613824 | tf_op jit(solution)/shard_map/ab,bpyx->apyx/dot_general | solution.py:14
  66.6 2.0 %convolution_add_fusion.9 = f32[2,2,128,286]{2,3,1,0:T(8,128)} fusion(f32[2,2,128,286]{2,3,1,0:T(8,128)S(1)} %fusion.46, f32[286,2,2,128]{3,2,1,0:T(2,128)S(1)} %get-tuple-element.46, f32[3,286,286]{2,1,0:T(8,128)S(1)} %copy-done.5), kind=kOutput, calls=%fused_computation.19 | convolution fusion | flops 502701056 | bytes 2203648 | tf_op jit(solution)/shard_map/ab,bpyx->apyx/dot_general | solution.py:14
  68.6 2.3 %convolution_add_fusion.3 = f32[2,2,128,286]{2,3,1,0:T(8,128)S(1)} fusion(f32[2,2,128,286]{2,3,1,0:T(8,128)S(1)} %convolution_add_fusion.4, f32[286,2,1,128]{3,0,2,1:T(8,128)S(1)} %copy.195, f32[286,2,1,128]{3,0,2,1:T(8,128)} %copy.196, f32[3,286,286]{2,1,0:T(8,128)S(1)} %copy-done.3, f32[286,2,128]{2,0,1:T(8,128)} %bitcast.37, ...), kind=kOutput, calls=%fused_computation.12 | convolution fusion | flops 503140352 | bytes 3084800 | tf_op jit(solution)/shard_map/ba,bpyx->apyx/dot_general | solution.py:18
  71.0 2.3 %convolution_add_fusion.2 = f32[2,2,128,286]{2,3,1,0:T(8,128)S(1)} fusion(f32[2,2,128,286]{2,3,1,0:T(8,128)S(1)} %convolution_add_fusion.3, f32[286,2,1,128]{3,0,2,1:T(8,128)S(1)} %copy.195, f32[286,2,1,128]{3,0,2,1:T(8,128)} %copy.196, f32[3,286,286]{2,1,0:T(8,128)S(1)} %copy-done.5, f32[286,2,128]{2,0,1:T(8,128)} %bitcast.39, ...), kind=kOutput, calls=%fused_computation.11 | convolution fusion | flops 503140352 | bytes 3084800 | tf_op jit(solution)/shard_map/ba,bpyx->apyx/dot_general | solution.py:18
  73.3 1.2 %convolution_add_fusion.1 = f32[2,2,128,286]{2,3,1,0:T(8,128)S(1)} fusion(f32[2,2,128,286]{2,3,1,0:T(8,128)S(1)} %convolution_add_fusion.2, f32[286,2,2,128]{3,2,1,0:T(2,128)S(1)} %get-tuple-element.33, f32[3,286,286]{2,1,0:T(8,128)S(1)} %copy-done.3), kind=kOutput, calls=%fused_computation.10 | convolution fusion | flops 502701056 | bytes 2203648 | tf_op jit(solution)/shard_map/ba,bpyx->apyx/dot_general | solution.py:18
  74.5 0.0 copy-start.14
  74.5 1.2 %fusion.11 = f32[286,2,2,128]{3,0,2,1:T(8,128)S(1)} fusion(f32[2,2,128,286]{2,3,1,0:T(8,128)S(1)} %convolution_add_fusion.1, f32[286,2,2,128]{3,2,1,0:T(2,128)S(1)} %get-tuple-element.32, f32[3,286,286]{2,1,0:T(8,128)S(1)} %copy-done.5), kind=kOutput, calls=%fused_computation.23 | convolution fusion | flops 502701056 | bytes 2203648 | tf_op jit(solution)/shard_map/ba,bpyx->apyx/dot_general | solution.py:18
  75.7 0.8 copy-done.17
  76.5 2.3 %fusion.33 = f32[35,2,2,128]{3,0,2,1:T(8,128)S(1)} fusion(f32[35,2,2,128]{3,0,2,1:T(8,128)S(1)} %copy.113, f32[35,2,2,128]{3,0,2,1:T(8,128)S(1)} %copy.87, f32[35,35,35]{2,1,0:T(8,128)S(1)} %copy-done.14, f32[35,35,35]{1,2,0:T(8,128)S(1)} %copy-done.16, f32[286,2,2,128]{3,0,2,1:T(8,128)S(1)} %fusion.11), kind=kOutput, calls=%fused_computation.34 | convolution fusion | flops 264129920 | bytes 629720 | tf_op jit(solution)/shard_map/kij,kjpyx->ipyx/dot_general | solution.py:85
  78.8 1.6 %scatter-add.9 = f32[286,2,2,128]{3,0,2,1:T(8,128)} dynamic-update-slice(f32[286,2,2,128]{3,0,2,1:T(8,128)} %copy-done.17, f32[35,2,2,128]{3,0,2,1:T(8,128)S(1)} %fusion.33, s32[]{:T(128)} %constant.51.clone.1, s32[]{:T(128)} %constant.51.clone.1, s32[]{:T(128)} %constant.51.clone.1, s32[]{:T(128)} %constant.51.clone.1) | dynamic-update-slice | bytes 143364 | tf_op jit(solution)/shard_map/scatter-add | solution.py:89
  80.5 2.6 %fusion.13 = f32[286,2,2,128]{3,0,2,1:T(8,128)S(1)} fusion(f32[286,2,2,128]{3,0,2,1:T(8,128)} %scatter-add.9, f32[286,2,2,128]{3,0,2,1:T(8,128)} %fusion.14, f32[286,286]{1,0:T(8,128)S(1)} %copy-done, f32[286]{0:T(512)S(1)} %copy-done.33, f32[2,2,128]{2,1,0:T(2,128)S(1)} %convert_element_type.4, f32[286,2,2,128]{3,2,1,0:T(2,128)S(1)} %copy-done.1), kind=kOutput, calls=%fused_computation.25 | convolution fusion | flops 503433216 | bytes 2673288 | tf_op jit(solution)/shard_map/ba,bpyx->apyx/dot_general | solution.py:18
  83.1 1.3 %copy.118 = f32[286,2,2,128]{3,2,1,0:T(2,128)} copy(f32[286,2,2,128]{3,0,2,1:T(8,128)S(1)} %fusion.13) | data formatting | bytes 1171456
  84.4 2.5 %convolution_add_fusion.8 = f32[2,2,128,286]{2,3,1,0:T(8,128)S(1)} fusion(f32[2,2,128,286]{2,3,1,0:T(8,128)S(1)} %copy-done.20, f32[286,2,1,128]{3,0,2,1:T(8,128)} %copy.193, f32[286,2,1,128]{3,0,2,1:T(8,128)} %copy.194, f32[3,286,286]{2,1,0:T(8,128)S(1)} %copy-done.3, f32[286,2,128]{2,0,1:T(8,128)} %bitcast.8, pred[2]{0:T(512)(128)(4,1)S(1)} %iota_compare_fusion.1, ...), kind=kOutput, calls=%fused_computation.18 | convolution fusion | flops 503140352 | bytes 3082752 | tf_op jit(solution)/shard_map/ab,bpyx->apyx/dot_general | solution.py:14
  86.9 2.4 %convolution_add_fusion.7 = f32[2,2,128,286]{2,3,1,0:T(8,128)S(1)} fusion(f32[2,2,128,286]{2,3,1,0:T(8,128)S(1)} %convolution_add_fusion.8, f32[286,2,1,128]{3,0,2,1:T(8,128)} %copy.193, f32[286,2,1,128]{3,0,2,1:T(8,128)} %copy.194, f32[3,286,286]{2,1,0:T(8,128)S(1)} %copy-done.6, f32[286,2,128]{2,0,1:T(8,128)} %bitcast.12, ...), kind=kOutput, calls=%fused_computation.17 | convolution fusion | flops 503140352 | bytes 3082752 | tf_op jit(solution)/shard_map/ab,bpyx->apyx/dot_general | solution.py:14
  89.4 0.0 copy-start.18
  89.4 1.2 %convolution_add_fusion.6 = f32[2,2,128,286]{2,3,1,0:T(8,128)S(1)} fusion(f32[2,2,128,286]{2,3,1,0:T(8,128)S(1)} %convolution_add_fusion.7, f32[286,2,2,128]{3,2,1,0:T(2,128)S(1)} %copy-done.19, f32[3,286,286]{2,1,0:T(8,128)S(1)} %copy-done.3), kind=kOutput, calls=%fused_computation.16 | convolution fusion | flops 502701056 | bytes 2203648 | tf_op jit(solution)/shard_map/ab,bpyx->apyx/dot_general | solution.py:14
  90.6 0.0 copy-start.15
  90.6 1.2 %fusion.8 = f32[286,2,2,128]{3,0,2,1:T(8,128)S(1)} fusion(f32[2,2,128,286]{2,3,1,0:T(8,128)S(1)} %convolution_add_fusion.6, f32[286,2,2,128]{3,2,1,0:T(2,128)S(1)} %copy-done.18, f32[3,286,286]{2,1,0:T(8,128)S(1)} %copy-done.6), kind=kOutput, calls=%fused_computation.20 | convolution fusion | flops 502701056 | bytes 2203648 | tf_op jit(solution)/shard_map/ab,bpyx->apyx/dot_general | solution.py:14
  91.8 2.4 %fusion.24 = f32[35,2,2,128]{3,0,2,1:T(8,128)S(1)} fusion(f32[35,2,2,128]{3,0,2,1:T(8,128)S(1)} %copy.87, f32[35,35,35,1,1]{2,1,0,4,3:T(8,128)S(1)} %bitcast.132, f32[286,2,2,128]{3,0,2,1:T(8,128)S(1)} %fusion.8), kind=kOutput, calls=%fused_computation.31 | convolution fusion | flops 264087040 | bytes 1034240 | tf_op jit(solution)/shard_map/kab,abpyx->kpyx/dot_general | solution.py:82
  94.1 0.3 scatter-add.6
  94.5 1.2 %fusion.10 = f32[286,2,2,128]{3,0,2,1:T(8,128)S(1)} fusion(f32[286,2,2,128]{3,0,2,1:T(8,128)S(1)} %scatter-add.6, f32[286,2,2,128]{3,0,2,1:T(8,128)S(1)} %copy-done.4, f32[286,286]{1,0:T(8,128)S(1)} %copy-done, f32[286,2,2,128]{3,2,1,0:T(2,128)S(1)} %copy-done.2), kind=kOutput, calls=%fused_computation.22 | convolution fusion | flops 503140352 | bytes 2670096 | tf_op jit(solution)/shard_map/ab,bpyx->apyx/dot_general | solution.py:14
  95.6 1.3 %copy.117 = f32[286,2,2,128]{3,2,1,0:T(2,128)} copy(f32[286,2,2,128]{3,0,2,1:T(8,128)S(1)} %fusion.10) | data formatting | bytes 1171456
  (75 shorter events, 0.2 us)
Async XLA Ops:
  0.6 79.9 %copy-start = (f32[286,286]{1,0:T(8,128)S(1)}, f32[286,286]{1,0:T(8,128)}, u32[]{:S(2)}) copy-start(f32[286,286]{1,0:T(8,128)} %param.23) | copy-start | bytes 981556
  0.6 9.8 %copy-start.1 = (f32[286,2,2,128]{3,2,1,0:T(2,128)S(1)}, f32[286,2,2,128]{3,2,1,0:T(2,128)}, u32[]{:S(2)}) copy-start(f32[286,2,2,128]{3,2,1,0:T(2,128)} %param.16) | copy-start | bytes 1757188
  2.8 8.9 %copy-start.7 = (f32[286,2,2,1]{3,2,1,0:T(2,128)}, f32[286,2,2,1]{3,2,1,0:T(2,128)S(1)}, u32[]{:S(2)}) copy-start(f32[286,2,2,1]{3,2,1,0:T(2,128)S(1)} %get-tuple-element.42) | copy-start | bytes 13732
  2.8 8.9 %copy-start.8 = (f32[286,2,2,1]{3,2,1,0:T(2,128)}, f32[286,2,2,1]{3,2,1,0:T(2,128)S(1)}, u32[]{:S(2)}) copy-start(f32[286,2,2,1]{3,2,1,0:T(2,128)S(1)} %get-tuple-element.43) | copy-start | bytes 13732
  2.8 14.4 %copy-start.2 = (f32[286,2,2,128]{3,2,1,0:T(2,128)S(1)}, f32[286,2,2,128]{3,2,1,0:T(2,128)}, u32[]{:S(2)}) copy-start(f32[286,2,2,128]{3,2,1,0:T(2,128)} %param.15) | copy-start | bytes 1757188
  3.2 36.2 %collective-permute-start.4 = (f32[286,2,2,1]{0,2,3,1:T(2,128)S(1)}, f32[286,2,2,1]{0,2,3,1:T(2,128)S(1)}, u32[]{:S(2)}, u32[]{:S(2)}) collective-permute-start(f32[286,2,2,1]{0,2,3,1:T(2,128)S(1)} %copy.149), channel_id=1, source_target_pairs={{16,0},{32,16},{48,32},{64,48},{80,64},{96,80},{112,96},{128,112},... | collective-permute-start | bytes 13736 | tf_op jit(solution)/shard_map/ppermute | solution.py:10
  8.5 33.7 %collective-permute-start.5 = (f32[286,2,2,1]{0,2,3,1:T(2,128)S(1)}, f32[286,2,2,1]{0,2,3,1:T(2,128)S(1)}, u32[]{:S(2)}, u32[]{:S(2)}) collective-permute-start(f32[286,2,2,1]{0,2,3,1:T(2,128)S(1)} %copy.150), channel_id=1, source_target_pairs={{0,16},{16,32},{32,48},{48,64},{64,80},{80,96},{96,112},{112,128},... | collective-permute-start | bytes 13736 | tf_op jit(solution)/shard_map/ppermute | solution.py:10
  11.7 56.9 %collective-permute-start.6 = (f32[286,2,1,128]{3,0,2,1:T(8,128)S(1)}, f32[286,2,1,128]{3,0,2,1:T(8,128)}, u32[]{:S(2)}, u32[]{:S(2)}) collective-permute-start(f32[286,2,1,128]{3,0,2,1:T(8,128)S(1)} %copy.195), channel_id=1, source_target_pairs={{1,0},{2,1},{3,2},{4,3},{5,4},{6,5},{7,6},{8,7},{9,8},{10,9},{11,1... | collective-permute-start | bytes 878600 | tf_op jit(solution)/shard_map/ppermute | solution.py:10
  18.0 10.3 %copy-start.9 = (f32[286,2,2,1]{3,2,1,0:T(2,128)}, f32[286,2,2,1]{3,2,1,0:T(2,128)S(1)}, u32[]{:S(2)}) copy-start(f32[286,2,2,1]{3,2,1,0:T(2,128)S(1)} %get-tuple-element.54) | copy-start | bytes 13732
  18.0 10.3 %copy-start.11 = (f32[286,2,2,1]{3,2,1,0:T(2,128)}, f32[286,2,2,1]{3,2,1,0:T(2,128)S(1)}, u32[]{:S(2)}) copy-start(f32[286,2,2,1]{3,2,1,0:T(2,128)S(1)} %get-tuple-element.55) | copy-start | bytes 13732
  18.4 26.6 %collective-permute-start = (f32[286,2,2,1]{0,2,3,1:T(2,128)S(1)}, f32[286,2,2,1]{0,2,3,1:T(2,128)S(1)}, u32[]{:S(2)}, u32[]{:S(2)}) collective-permute-start(f32[286,2,2,1]{0,2,3,1:T(2,128)S(1)} %copy.147), channel_id=1, source_target_pairs={{0,16},{16,32},{32,48},{48,64},{64,80},{80,96},{96,112},{112,128},... | collective-permute-start | bytes 13736 | tf_op jit(solution)/shard_map/ppermute | solution.py:10
  20.7 32.1 %collective-permute-start.1 = (f32[286,2,2,1]{0,2,3,1:T(2,128)S(1)}, f32[286,2,2,1]{0,2,3,1:T(2,128)S(1)}, u32[]{:S(2)}, u32[]{:S(2)}) collective-permute-start(f32[286,2,2,1]{0,2,3,1:T(2,128)S(1)} %copy.148), channel_id=1, source_target_pairs={{16,0},{32,16},{48,32},{64,48},{80,64},{96,80},{112,96},{128,112},... | collective-permute-start | bytes 13736 | tf_op jit(solution)/shard_map/ppermute | solution.py:10
  31.2 2.3 %copy-start.29 = (f32[3,286]{1,0:T(4,128)S(1)}, f32[3,286]{1,0:T(4,128)}, u32[]{:S(2)}) copy-start(f32[3,286]{1,0:T(4,128)} %param.21) | copy-start | bytes 10300
  31.2 2.3 %copy-start.30 = (f32[286]{0:T(512)S(1)}, f32[286]{0:T(512)}, u32[]{:S(2)}) copy-start(f32[286]{0:T(512)} %param.20) | copy-start | bytes 3436
  31.2 2.3 %copy-start.31 = (s32[2,2,128]{2,1,0:T(2,128)S(1)}, s32[2,2,128]{2,1,0:T(2,128)}, u32[]{:S(2)}) copy-start(s32[2,2,128]{2,1,0:T(2,128)} %param.24) | copy-start | bytes 6148
  31.3 3.7 %copy-start.27 = (f32[286,2,1,128]{3,2,1,0:T(1,128)S(1)}, f32[286,2,1,128]{3,2,1,0:T(1,128)}, u32[]{:S(2)}) copy-start(f32[286,2,1,128]{3,2,1,0:T(1,128)} %get-tuple-element.40) | copy-start | bytes 878596
  32.3 3.4 %slice-start.1 = ((f32[286,2,2,128]{3,2,1,0:T(2,128)}), f32[35,2,2,128]{3,2,1,0:T(2,128)S(1)}, s32[]{:S(2)}) async-start(f32[286,2,2,128]{3,2,1,0:T(2,128)} %param.15), calls=%async_computation.1 | async-start | bytes 143360 | tf_op jit(solution)/shard_map/slice | solution.py:79
  32.3 3.4 %copy-start.13 = (f32[35,35,35]{2,1,0:T(8,128)S(1)}, f32[35,35,35]{2,1,0:T(8,128)}, u32[]{:S(2)}) copy-start(f32[35,35,35]{2,1,0:T(8,128)} %param.19) | copy-start | bytes 514504
  34.9 2.0 %slice-start = ((f32[286,2,2,128]{3,2,1,0:T(2,128)}), f32[35,2,2,128]{3,2,1,0:T(2,128)S(1)}, s32[]{:S(2)}) async-start(f32[286,2,2,128]{3,2,1,0:T(2,128)} %param.16), calls=%async_computation | async-start | bytes 143360 | tf_op jit(solution)/shard_map/slice | solution.py:80
  34.9 2.0 %copy-start.32 = (s32[2,2,128]{2,1,0:T(2,128)S(1)}, s32[2,2,128]{2,1,0:T(2,128)}, u32[]{:S(2)}) copy-start(s32[2,2,128]{2,1,0:T(2,128)} %param.25) | copy-start | bytes 6148
  35.7 3.0 %copy-start.28 = (f32[286,2,1,128]{3,2,1,0:T(1,128)S(1)}, f32[286,2,1,128]{3,2,1,0:T(1,128)}, u32[]{:S(2)}) copy-start(f32[286,2,1,128]{3,2,1,0:T(1,128)} %get-tuple-element.51) | copy-start | bytes 878596
  39.4 31.6 %collective-permute-start.7 = (f32[286,2,1,128]{3,0,2,1:T(8,128)}, f32[286,2,1,128]{3,0,2,1:T(8,128)}, u32[]{:S(2)}, u32[]{:S(2)}) collective-permute-start(f32[286,2,1,128]{3,0,2,1:T(8,128)} %copy.196), channel_id=1, source_target_pairs={{0,1},{1,2},{2,3},{3,4},{4,5},{5,6},{6,7},{7,8},{8,9},{9,10},{10,1... | collective-permute-start | bytes 878600 | tf_op jit(solution)/shard_map/ppermute | solution.py:10
  42.2 42.2 %collective-permute-start.2 = (f32[286,2,1,128]{3,0,2,1:T(8,128)}, f32[286,2,1,128]{3,0,2,1:T(8,128)}, u32[]{:S(2)}, u32[]{:S(2)}) collective-permute-start(f32[286,2,1,128]{3,0,2,1:T(8,128)} %copy.194), channel_id=1, source_target_pairs={{0,1},{1,2},{2,3},{3,4},{4,5},{5,6},{6,7},{7,8},{8,9},{9,10},{10,1... | collective-permute-start | bytes 878600 | tf_op jit(solution)/shard_map/ppermute | solution.py:10
  45.0 41.8 %collective-permute-start.3 = (f32[286,2,1,128]{3,0,2,1:T(8,128)}, f32[286,2,1,128]{3,0,2,1:T(8,128)}, u32[]{:S(2)}, u32[]{:S(2)}) collective-permute-start(f32[286,2,1,128]{3,0,2,1:T(8,128)} %copy.193), channel_id=1, source_target_pairs={{1,0},{2,1},{3,2},{4,3},{5,4},{6,5},{7,6},{8,7},{9,8},{10,9},{11,1... | collective-permute-start | bytes 878600 | tf_op jit(solution)/shard_map/ppermute | solution.py:10
  53.8 5.4 %copy-start.3 = (f32[3,286,286]{2,1,0:T(8,128)S(1)}, f32[3,286,286]{2,1,0:T(8,128)}, u32[]{:S(2)}) copy-start(f32[3,286,286]{2,1,0:T(8,128)} %param.17) | copy-start | bytes 2944660
  53.8 7.9 %copy-start.23 = (f32[286,1,2,128]{3,2,1,0:T(2,128)S(1)}, f32[286,1,2,128]{3,2,1,0:T(2,128)}, u32[]{:S(2)}) copy-start(f32[286,1,2,128]{3,2,1,0:T(2,128)} %get-tuple-element.48) | copy-start | bytes 878596
  53.8 7.9 %copy-start.24 = (f32[286,1,2,128]{3,2,1,0:T(2,128)S(1)}, f32[286,1,2,128]{3,2,1,0:T(2,128)}, u32[]{:S(2)}) copy-start(f32[286,1,2,128]{3,2,1,0:T(2,128)} %get-tuple-element.49) | copy-start | bytes 878596
  53.8 7.9 %copy-start.25 = (f32[286,2,2]{2,1,0:T(2,128)S(1)}, f32[286,2,2]{2,1,0:T(2,128)}, u32[]{:S(2)}) copy-start(f32[286,2,2]{2,1,0:T(2,128)} %copy.74) | copy-start | bytes 13732
  53.8 7.9 %copy-start.26 = (f32[286,2,2]{2,1,0:T(2,128)S(1)}, f32[286,2,2]{2,1,0:T(2,128)}, u32[]{:S(2)}) copy-start(f32[286,2,2]{2,1,0:T(2,128)} %copy.78) | copy-start | bytes 13732
  59.2 1.3 %copy-start.5 = (f32[3,286,286]{2,1,0:T(8,128)S(1)}, f32[3,286,286]{2,1,0:T(8,128)}, u32[]{:S(2)}) copy-start(f32[3,286,286]{2,1,0:T(8,128)} %param.18) | copy-start | bytes 2944660
  59.2 2.5 %copy-start.22 = (f32[286,2,2,127]{3,2,1,0:T(2,128)S(1)}, f32[286,2,2,127]{3,2,1,0:T(2,128)}, u32[]{:S(2)}) copy-start(f32[286,2,2,127]{3,2,1,0:T(2,128)} %get-tuple-element.53) | copy-start | bytes 1743460
  60.4 1.4 %copy-start.10 = (f32[286,2,2,1]{3,2,1,0:T(2,128)S(1)}, f32[286,2,2,1]{3,2,1,0:T(2,128)}, u32[]{:S(2)}) copy-start(f32[286,2,2,1]{3,2,1,0:T(2,128)} %copy-done.9) | copy-start | bytes 13732
  60.4 1.4 %copy-start.12 = (f32[286,2,2,1]{3,2,1,0:T(2,128)S(1)}, f32[286,2,2,1]{3,2,1,0:T(2,128)}, u32[]{:S(2)}) copy-start(f32[286,2,2,1]{3,2,1,0:T(2,128)} %copy-done.11) | copy-start | bytes 13732
  60.5 1.4 %copy-start.21 = (f32[286,2,2,127]{3,2,1,0:T(2,128)S(1)}, f32[286,2,2,127]{3,2,1,0:T(2,128)}, u32[]{:S(2)}) copy-start(f32[286,2,2,127]{3,2,1,0:T(2,128)} %get-tuple-element.52) | copy-start | bytes 1743460
  74.5 2.0 %copy-start.14 = (f32[35,35,35]{2,1,0:T(8,128)S(1)}, f32[35,35,35]{2,1,0:T(8,128)}, u32[]{:S(2)}) copy-start(f32[35,35,35]{2,1,0:T(8,128)} %param.19) | copy-start | bytes 514504
  74.5 2.0 %copy-start.16 = (f32[35,35,35]{1,2,0:T(8,128)S(1)}, f32[35,35,35]{1,2,0:T(8,128)}, u32[]{:S(2)}) copy-start(f32[35,35,35]{1,2,0:T(8,128)} %copy.112) | copy-start | bytes 514504
  75.7 0.8 copy-start.17
  76.5 3.9 %copy-start.33 = (f32[286]{0:T(512)S(1)}, f32[286]{0:T(512)}, u32[]{:S(2)}) copy-start(f32[286]{0:T(512)} %param.22) | copy-start | bytes 3436
  80.5 3.9 %copy-start.20 = (f32[2,2,128,286]{2,3,1,0:T(8,128)S(1)}, f32[2,2,128,286]{2,3,1,0:T(8,128)}, u32[]{:S(2)}) copy-start(f32[2,2,128,286]{2,3,1,0:T(8,128)} %convolution_add_fusion.9) | copy-start | bytes 1757188
  84.4 2.5 %copy-start.6 = (f32[3,286,286]{2,1,0:T(8,128)S(1)}, f32[3,286,286]{2,1,0:T(8,128)}, u32[]{:S(2)}) copy-start(f32[3,286,286]{2,1,0:T(8,128)} %param.18) | copy-start | bytes 2944660
  86.9 2.5 %copy-start.19 = (f32[286,2,2,128]{3,2,1,0:T(2,128)S(1)}, f32[286,2,2,128]{3,2,1,0:T(2,128)}, u32[]{:S(2)}) copy-start(f32[286,2,2,128]{3,2,1,0:T(2,128)} %get-tuple-element.35) | copy-start | bytes 1757188
  89.4 1.2 %copy-start.18 = (f32[286,2,2,128]{3,2,1,0:T(2,128)S(1)}, f32[286,2,2,128]{3,2,1,0:T(2,128)}, u32[]{:S(2)}) copy-start(f32[286,2,2,128]{3,2,1,0:T(2,128)} %get-tuple-element.34) | copy-start | bytes 1757188
  90.6 1.2 %copy-start.15 = (f32[35,35,35]{2,1,0:T(8,128)S(1)}, f32[35,35,35]{2,1,0:T(8,128)}, u32[]{:S(2)}) copy-start(f32[35,35,35]{2,1,0:T(8,128)} %param.19) | copy-start | bytes 514504
  91.8 2.7 %copy-start.4 = (f32[286,2,2,128]{3,0,2,1:T(8,128)S(1)}, f32[286,2,2,128]{3,0,2,1:T(8,128)}, u32[]{:S(2)}) copy-start(f32[286,2,2,128]{3,0,2,1:T(8,128)} %fusion.14) | copy-start | bytes 1757188
where the time goes:
time: 97.6 us; the launch traced here: 96.9 us
  starting transfers between devices  30.9 us (32%)
  matrix products  29.6 us (30%)
  local copies, waits for them, and re-layouts  26.3 us (27%)
  other arithmetic  8.94 us (9%)
  between operations  1.24 us (1%)
    ppermute x8, starting transfers between devices, from_behind(): return lax.ppermute(block, axis, route)  30.9 us
    dot_general x7, matrix products, apply_transposed(): jnp.einsum('ba,bpyx->apyx', matrix, field, precision=lax.Precision.HIGHEST)  12 us
    dot_general x7, matrix products, apply_matrix(): jnp.einsum('ab,bpyx->apyx', matrix, field, precision=lax.Precision.HIGHEST)  11.6 us
    unnamed x79, local copies, waits for them, and re-layouts  9.59 us
    sub x1, other arithmetic, on_device(): adminus[direction] - adjoint  5.37 us
    sub x1, other arithmetic, on_device(): plus_all[direction] - state  3.55 us
    dot_general x1, matrix products, on_device(): jnp.einsum('kab,abpyx->kpyx', collision, products, precision=lax.Precisio...  2.35 us
    dot_general x1, matrix products, on_device(): jnp.einsum('kij,kjpyx->ipyx', symmetric, cross, precision=lax.Precision.H...  2.29 us
  transfers between devices with their start and end apart: 8, of which 0 were waited for; matrix products, arithmetic and copies ran while one was open for 53% of the time, Pallas kernels for 0%

commit v1 on v0

v1 whole, which is shorter than its diff:
```python
import jax
import jax.numpy as jnp
from jax import lax
from jax.experimental import pallas as pl
from jax.experimental.pallas import tpu as pltpu
from jax.sharding import PartitionSpec as P

F32 = jnp.float32
BF16 = jnp.bfloat16


def both_ways(pairs):
    return [(i, j) for i, j in pairs] + [(j, i) for i, j in pairs]


def split(x):
    hi = x.astype(BF16)
    lo = (x - hi.astype(F32)).astype(BF16)
    return hi, lo


def contract(a, b, left):
    return lax.dot_general(a, b, (((left,), (0,)), ((), ())), preferred_element_type=F32)


def dot3(a, b, left=1):
    return contract(a[0], b[0], left) + (contract(a[0], b[1], left) + contract(a[1], b[0], left))


def pack_kernel(par_ref, s_ref, a_ref, e_ref, o_ref, xe_ref, xo_ref):
    m, half = s_ref.shape[0] // 4, e_ref.shape[0] // 2
    py, px = par_ref[0] & 1, par_ref[0] >> 1
    lanes = lax.broadcasted_iota(jnp.int32, (m, 128), 1)
    last = jnp.zeros((m, 128), F32)
    first = jnp.zeros((m, 128), F32)
    for f, ref in enumerate((s_ref, a_ref)):
        for z in range(2):
            rows = [ref[pl.ds(2 * z + y, m, stride=4), :] for y in range(2)]
            here = (pl.ds(f * half, m), pl.ds(z * 128, 128))
            e_ref[here] = jnp.where(py == 0, rows[1], rows[0])
            o_ref[here] = jnp.where(py == 0, rows[0], rows[1])
            for y in range(2):
                j = f * 4 + 2 * z + y
                last = jnp.where(lanes == j, pltpu.roll(rows[y], j + 1, 1), last)
                col = rows[y] if j == 0 else pltpu.roll(rows[y], j, 1)
                first = jnp.where(lanes == j, col, first)
    xe_ref[...] = jnp.where(px == 0, last, first)
    xo_ref[...] = jnp.where(px == 0, first, last)


def interior_kernel(
    par_ref, s_ref, a_ref, xe_ref, xo_ref, up_ref, un_ref, col_ref, relax_ref, wt_ref, dw_ref,
    codes_ref, mask_ref, rs_ref, ra_ref, tab_ref, gain_ref,
):
    m = rs_ref.shape[1]
    low = col_ref.shape[0]
    px = par_ref[0] >> 1
    lanes = lax.broadcasted_iota(jnp.int32, (m, 128), 1)
    xe, xo = xe_ref[...], xo_ref[...]
    xm_all = jnp.where(px == 0, xo, xe)
    xp_all = jnp.where(px == 0, xe, xo)

    def wide(blocks):
        return jnp.concatenate(blocks, axis=1)

    tab_ref[...] = jnp.zeros_like(tab_ref)
    tab_ref[0:1, :] = relax_ref[...]
    tab_ref[1:4, :] = wt_ref[...]
    tab_ref[4:5, :] = dw_ref[...]
    thi, tlo = split(tab_ref[...])
    codes = [codes_ref[q : q + 1, :] for q in range(4)]
    walls = [mask_ref[q : q + 1, :] for q in range(4)]
    sub = lax.broadcasted_iota(jnp.int32, (8, 128), 0)

    def damp_of(row):
        pick = wide([
            jnp.where((sub == 0) | ((sub > 0) & (sub < 4) & (codes[2 * z + row] == sub)), 1.0, 0.0)
            for z in range(2)
        ]).astype(BF16)
        return contract(thi, pick, 0) + contract(tlo, pick, 0)

    def source_of(row):
        pick = wide([jnp.where((sub == 4) & (walls[2 * z + row] != 0), 1.0, 0.0) for z in range(2)]).astype(BF16)
        return contract(thi, pick, 0) + contract(tlo, pick, 0)

    damp = [damp_of(r) for r in range(2)]

    def low_of(ref):
        return wide([ref[pl.ds(2 * z + y, low, stride=4), :] for y in range(2) for z in range(2)])

    s_low, a_low = low_of(s_ref), low_of(a_ref)
    s_low2 = split(s_low)
    adgain = jnp.zeros((low, 512), F32)
    for k in range(low):
        c = col_ref[k]
        u = dot3(split(c + c.T), s_low2)
        adgain = adgain + a_low[k : k + 1, :] * u
        gain_ref[k : k + 1, :] = 0.5 * jnp.sum(s_low * u, axis=0, keepdims=True)
    gain = gain_ref[...]

    pos = [up_ref[d] for d in range(3)]
    neg = [un_ref[d] for d in range(3)]
    pos_x, neg_x = split(pos[0]), split(neg[0])
    pos_y, neg_y = split(pos[1]), split(neg[1])
    diff_z = split(pos[2] - neg[2])

    for f, (ref, out_ref) in enumerate(((s_ref, rs_ref), (a_ref, ra_ref))):
        blk = [[ref[pl.ds(2 * z + y, m, stride=4), :] for z in range(2)] for y in range(2)]
        behind, ahead = [], []
        for y in range(2):
            bs, hs = [], []
            for z in range(2):
                j = f * 4 + 2 * z + y
                b = blk[y][z]
                xm = xm_all if j == 0 else pltpu.roll(xm_all, 128 - j, 1)
                xp = pltpu.roll(xp_all, 127 - j, 1)
                bs.append(b - jnp.where(lanes == 0, xm, pltpu.roll(b, 1, 1)))
                hs.append(jnp.where(lanes == 127, xp, pltpu.roll(b, 127, 1)) - b)
            behind.append(split(wide(bs)))
            ahead.append(split(wide(hs)))
        step_y = split(wide([blk[1][z] - blk[0][z] for z in range(2)]))
        step_z = split(wide([blk[y][0] - blk[y][1] for y in range(2)]))
        if f == 0:
            zpart = dot3(diff_z, step_z)
            rows = [
                dot3(pos_x, behind[0]) + dot3(neg_x, ahead[0]) + dot3(neg_y, step_y),
                dot3(pos_x, behind[1]) + dot3(neg_x, ahead[1]) + dot3(pos_y, step_y),
            ]
        else:
            zpart = dot3(diff_z, step_z, 0)
            rows = [
                -(dot3(pos_x, ahead[0], 0) + dot3(neg_x, behind[0], 0) + dot3(pos_y, step_y, 0)),
                -(dot3(pos_x, ahead[1], 0) + dot3(neg_x, behind[1], 0) + dot3(neg_y, step_y, 0)),
            ]
        for y in range(2):
            zrow = zpart[:, y * 128 : (y + 1) * 128]
            res = rows[y] + wide([zrow, -zrow]) + damp[y] * wide(blk[y])
            if f == 1:
                res = res - source_of(y)
            out_ref[y] = res
            g = gain if f == 0 else adgain
            out_ref[y, 0:low, :] = out_ref[y, 0:low, :] - g[:, y * 256 : (y + 1) * 256]


def finish_row(row, own_ref, recv_ref, rs_ref, ra_ref, up_ref, un_ref, b_ref):
    m, half = rs_ref.shape[1], own_ref.shape[0] // 2
    sign = jnp.where(row == 1, 1.0, -1.0).astype(F32)
    own_s, own_a = own_ref[0:m, :], own_ref[half : half + m, :]
    pos, neg = up_ref[0], un_ref[0]
    with_s = split(jnp.where(row == 1, neg, pos))
    with_a = split(jnp.where(row == 1, pos, neg))
    inverse = split(b_ref[...])
    res_s = rs_ref[0] + dot3(with_s, split(sign * (recv_ref[0:m, :] - own_s)))
    new_s = own_s - 0.5 * dot3(inverse, split(res_s))
    res_a = ra_ref[0] + dot3(with_a, split(sign * (own_a - recv_ref[half : half + m, :])), 0)
    new_a = own_a - 0.5 * dot3(inverse, split(res_a), 0)
    return new_s, new_a


def first_kernel(row_ref, own_ref, recv_ref, rs_ref, ra_ref, up_ref, un_ref, b_ref, out_ref):
    out_ref[0], out_ref[1] = finish_row(row_ref[0], own_ref, recv_ref, rs_ref, ra_ref, up_ref, un_ref, b_ref)


def last_kernel(row_ref, own_ref, recv_ref, rs_ref, ra_ref, up_ref, un_ref, b_ref, done_ref, s_ref, a_ref):
    m = rs_ref.shape[1]
    new = finish_row(row_ref[0], own_ref, recv_ref, rs_ref, ra_ref, up_ref, un_ref, b_ref)
    for f, ref in enumerate((s_ref, a_ref)):
        for z in range(2):
            here = new[f][:, z * 128 : (z + 1) * 128]
            there = done_ref[f, :, z * 128 : (z + 1) * 128]
            ref[pl.ds(2 * z, m, stride=4), :] = jnp.where(row_ref[0] == 0, here, there)
            ref[pl.ds(2 * z + 1, m, stride=4), :] = jnp.where(row_ref[0] == 0, there, here)


def whole(shape):
    return pl.BlockSpec(shape, lambda *_: (0,) * len(shape))


def at_row(shape, index):
    return pl.BlockSpec((1,) + shape[1:], lambda i, row: (row[0] if index is None else index,) + (0,) * (len(shape) - 1))


PARAMS = pltpu.CompilerParams(vmem_limit_bytes=40 * 1024 * 1024)


def call(kernel, name, scalars, args, in_specs, outs, scratch=()):
    flat = jax.tree.leaves(outs)
    return pl.pallas_call(
        kernel,
        name=name,
        out_shape=outs,
        grid_spec=pltpu.PrefetchScalarGridSpec(
            num_scalar_prefetch=1,
            grid=(1,),
            in_specs=in_specs,
            out_specs=jax.tree.map(lambda o: whole(o.shape), outs),
            scratch_shapes=list(scratch),
        ),
        compiler_params=PARAMS,
    )(scalars, *args)


def on_device(
    state, adjoint, upwind_pos, upwind_neg, collision, relax, wall_table, drag_weights, block_inverse,
    cell_codes, wall_mask,
):
    m = state.shape[0]
    low = collision.shape[0]
    gy, gx = lax.axis_index("gy"), lax.axis_index("gx")
    ny, nx = lax.axis_size("gy"), lax.axis_size("gx")
    py, px = gy & 1, gx & 1
    par = (py + 2 * px).astype(jnp.int32).reshape(1)
    s = state.reshape(m * 4, 128)
    a = adjoint.reshape(m * 4, 128)
    rowbuf = jax.ShapeDtypeStruct((2, m, 256), F32)
    swapbuf = jax.ShapeDtypeStruct((2 * ((m + 7) // 8 * 8), 256), F32)
    colbuf = jax.ShapeDtypeStruct((m, 128), F32)
    own_e, own_o, send_xe, send_xo = call(
        pack_kernel, "pack", par, (s, a), [whole(s.shape)] * 2, (swapbuf, swapbuf, colbuf, colbuf)
    )
    even = lambda n: both_ways([(i, i + 1) for i in range(0, n - 1, 2)])
    odd = lambda n: both_ways([(i, i + 1) for i in range(1, n - 1, 2)])
    recv_o = lax.ppermute(own_o, "gy", odd(ny))
    recv_e = lax.ppermute(own_e, "gy", even(ny))
    recv_xe = lax.ppermute(send_xe, "gx", even(nx))
    recv_xo = lax.ppermute(send_xo, "gx", odd(nx))
    interior_args = (
        s, a, recv_xe, recv_xo, upwind_pos, upwind_neg, collision, relax.reshape(1, m), wall_table,
        drag_weights.reshape(1, m), cell_codes.reshape(4, 128), wall_mask.reshape(4, 128),
    )
    res_s, res_a = call(
        interior_kernel, "interior", par, interior_args, [whole(x.shape) for x in interior_args],
        (rowbuf, rowbuf),
        (pltpu.VMEM((8, m), F32), pltpu.VMEM((low, 512), F32)),
    )
    wshape = upwind_pos.shape
    row_specs = [
        whole(swapbuf.shape), whole(swapbuf.shape), at_row(rowbuf.shape, None), at_row(rowbuf.shape, None),
        at_row(wshape, 1), at_row(wshape, 1), whole(block_inverse.shape),
    ]
    tail = (res_s, res_a, upwind_pos, upwind_neg, block_inverse)
    row_e = (1 - py).astype(jnp.int32).reshape(1)
    row_o = py.astype(jnp.int32).reshape(1)
    done = call(first_kernel, "first", row_e, (own_e, recv_e) + tail, row_specs, rowbuf)
    out = jax.ShapeDtypeStruct(s.shape, F32)
    s_next, a_next = call(
        last_kernel, "last", row_o, (own_o, recv_o) + tail + (done,), row_specs + [whole(rowbuf.shape)], (out, out)
    )
    return s_next.reshape(state.shape), a_next.reshape(adjoint.shape)


def solution(mesh):
    field, cells = P(None, None, "gy", "gx"), P(None, "gy", "gx")
    in_specs = (field, field, P(), P(), P(), P(), P(), P(), P(), cells, cells)
    return jax.shard_map(
        on_device, mesh=mesh, in_specs=in_specs, out_specs=(field, field), check_vma=False
    )
```

time: 97.6 us -> 58.6 us (0.60)
  the two profiles are of different devices: /device:TPU:224 before, /device:TPU:102 now
where the time goes in v1:
time: 58.6 us; the launch traced here: 58.1 us
  waiting for transfers between devices  23.5 us (40%)
  starting transfers between devices  12.4 us (21%)
  Pallas kernels  12.1 us (21%)
  local copies, waits for them, and re-layouts  9.31 us (16%)
  between operations  0.74 us (1%)
    ppermute x1, waiting for transfers between devices, on_device(): recv_xo = lax.ppermute(send_xo, 'gx', odd(nx))  23.5 us
    pallas_call x4, Pallas kernels, call(): pl.pallas_call(kernel, name=name, out_shape=outs, grid_spec=pltpu.Prefetc...  12.1 us
    unnamed x26, local copies, waits for them, and re-layouts  7.94 us
    ppermute x1, starting transfers between devices, on_device(): recv_o = lax.ppermute(own_o, 'gy', odd(ny))  6.06 us
    ppermute x1, starting transfers between devices, on_device(): recv_xo = lax.ppermute(send_xo, 'gx', odd(nx))  5.46 us
  transfers between devices with their start and end apart: 4, of which 1 were waited for; matrix products, arithmetic and copies ran while one was open for 2% of the time, Pallas kernels for 14%

profile of v1, /device:TPU:102, one launch (start us, length us, event | category | flops | bytes accessed | tf_op | source)
XLA Modules:
  0.0 58.1 jit_solution(9424289083859054026)
XLA Ops:
  0.6 0.0 copy-start.4
  0.6 1.1 %copy-done.4 = f32[286,2,2,128]{3,2,1,0:T(2,128)S(1)} copy-done((f32[286,2,2,128]{3,2,1,0:T(2,128)S(1)}, f32[286,2,2,128]{3,2,1,0:T(2,128)}, u32[]{:S(2)}) %copy-start.4) | copy-done | bytes 585752
  1.7 0.0 copy-start.6
  1.7 1.1 %copy-done.6 = f32[286,2,2,128]{3,2,1,0:T(2,128)S(1)} copy-done((f32[286,2,2,128]{3,2,1,0:T(2,128)S(1)}, f32[286,2,2,128]{3,2,1,0:T(2,128)}, u32[]{:S(2)}) %copy-start.6) | copy-done | bytes 585752
  2.8 0.0 copy-start.5
  2.8 0.0 copy-start.7
  2.8 1.4 %pack.1 = (f32[576,256]{1,0:T(8,128)S(1)}, f32[576,256]{1,0:T(8,128)S(1)}, f32[286,128]{1,0:T(8,128)}, f32[286,128]{1,0:T(8,128)}) custom-call(s32[1]{0:T(128)} %bitcast.1.par_ref, f32[1144,128]{1,0:T(8,128)S(1)} %bitcast.9, f32[1144,128]{1,0:T(8,128)S(1)} %bitcast.11), custom_call_target="tpu_custom_call" | custom-call | tf_op jit(solution)/shard_map/pack/pallas_call | solution.py:188
  4.2 0.8 %collective-permute-start.3 = (f32[576,256]{1,0:T(8,128)S(1)}, f32[576,256]{1,0:T(8,128)S(1)}, u32[]{:S(2)}, u32[]{:S(2)}) collective-permute-start(f32[576,256]{1,0:T(8,128)S(1)} %get-tuple-element.15.own_ref), channel_id=1, source_target_pairs={{0,1},{2,3},{4,5},{6,7},{8,9},{10,11},{12,13},{14,15},{1,0},{3,2},... | collective-permute-start | bytes 1769480 | tf_op jit(solution)/shard_map/ppermute | solution.py:224
  5.0 6.1 %collective-permute-start = (f32[576,256]{1,0:T(8,128)S(1)}, f32[576,256]{1,0:T(8,128)S(1)}, u32[]{:S(2)}, u32[]{:S(2)}) collective-permute-start(f32[576,256]{1,0:T(8,128)S(1)} %get-tuple-element.10.own_ref), channel_id=1, source_target_pairs={{1,2},{3,4},{5,6},{7,8},{9,10},{11,12},{13,14},{2,1},{4,3},{6,5},{... | collective-permute-start | bytes 1769480 | tf_op jit(solution)/shard_map/ppermute | solution.py:223
  11.1 0.1 collective-permute-start.1
  11.2 5.5 %collective-permute-start.2 = (f32[286,128]{1,0:T(8,128)}, f32[286,128]{1,0:T(8,128)}, u32[]{:S(2)}, u32[]{:S(2)}) collective-permute-start(f32[286,128]{1,0:T(8,128)} %get-tuple-element.12), channel_id=1, source_target_pairs={{16,32},{48,64},{80,96},{112,128},{144,160},{176,192},{208,224},{3... | collective-permute-start | bytes 439304 | tf_op jit(solution)/shard_map/ppermute | solution.py:226
  16.6 0.7 %reshape.41.relax_ref = f32[1,286]{1,0:T(1,128)S(1)} reshape(f32[286]{0:T(512)} %param.16) | data formatting | bytes 2288 | tf_op jit(solution)/shard_map/reshape | solution.py:228
  17.3 0.7 %reshape.42.dw_ref = f32[1,286]{1,0:T(1,128)S(1)} reshape(f32[286]{0:T(512)} %param.18) | data formatting | bytes 2288 | tf_op jit(solution)/shard_map/reshape | solution.py:229
  18.0 0.0 collective-permute-done.1.xe_ref
  18.0 23.5 %collective-permute-done.2.xo_ref = f32[286,128]{1,0:T(8,128)} collective-permute-done((f32[286,128]{1,0:T(8,128)}, f32[286,128]{1,0:T(8,128)}, u32[]{:S(2)}, u32[]{:S(2)}) %collective-permute-start.2) | collective-permute-done | bytes 146464 | tf_op jit(solution)/shard_map/ppermute | solution.py:226
  41.5 0.0 copy-done.5
  41.5 0.0 copy-done.7
  41.5 0.0 copy-start
  41.5 1.3 %copy-done = f32[3,286,286]{2,1,0:T(8,128)S(1)} copy-done((f32[3,286,286]{2,1,0:T(8,128)S(1)}, f32[3,286,286]{2,1,0:T(8,128)}, u32[]{:S(2)}) %copy-start) | copy-done | bytes 981576
  42.9 0.0 copy-start.2
  42.9 1.3 %copy-done.2 = f32[3,286,286]{2,1,0:T(8,128)S(1)} copy-done((f32[3,286,286]{2,1,0:T(8,128)S(1)}, f32[3,286,286]{2,1,0:T(8,128)}, u32[]{:S(2)}) %copy-start.2) | copy-done | bytes 981576
  44.2 0.0 copy-start.9
  44.2 1.1 %copy-done.9 = f32[35,35,35]{2,1,0:T(8,128)S(1)} copy-done((f32[35,35,35]{2,1,0:T(8,128)S(1)}, f32[35,35,35]{2,1,0:T(8,128)}, u32[]{:S(2)}) %copy-start.9) | copy-done | bytes 171524
  45.3 0.0 copy-start.10
  45.3 0.7 %copy-done.10 = f32[3,286]{1,0:T(4,128)S(1)} copy-done((f32[3,286]{1,0:T(4,128)S(1)}, f32[3,286]{1,0:T(4,128)}, u32[]{:S(2)}) %copy-start.10) | copy-done | bytes 3456
  46.0 0.0 copy-start.11
  46.0 0.7 %copy-done.11 = s32[2,2,128]{2,1,0:T(2,128)S(1)} copy-done((s32[2,2,128]{2,1,0:T(2,128)S(1)}, s32[2,2,128]{2,1,0:T(2,128)}, u32[]{:S(2)}) %copy-start.11) | copy-done | bytes 2072
  46.7 0.0 copy-start.12
  46.7 0.7 %copy-done.12 = s32[2,2,128]{2,1,0:T(2,128)S(1)} copy-done((s32[2,2,128]{2,1,0:T(2,128)S(1)}, s32[2,2,128]{2,1,0:T(2,128)}, u32[]{:S(2)}) %copy-start.12) | copy-done | bytes 2072
  47.4 0.0 copy-start.1
  47.4 0.0 copy-start.3
  47.4 0.0 copy-start.8
  47.4 6.5 %interior.1 = (f32[2,286,256]{2,1,0:T(8,128)S(1)}, f32[2,286,256]{2,1,0:T(8,128)S(1)}) custom-call(s32[1]{0:T(128)} %bitcast.1.par_ref, f32[1144,128]{1,0:T(8,128)S(1)} %bitcast.10, f32[1144,128]{1,0:T(8,128)S(1)} %bitcast.12, f32[286,128]{1,0:T(8,128)} %collective-permute-done.1.xe_ref, f32[286,128]{1,0:T(8,128)} %collective-permute-done.2.xo_ref, ...), custom_call_target="tpu_custom_call" | custom-call | tf_op jit(solution)/shard_map/interior/pallas_call | solution.py:188
  53.9 0.0 collective-permute-done.3.recv_ref
  53.9 0.0 copy-done.1
  53.9 0.0 copy-done.3
  53.9 0.0 copy-done.8
  53.9 1.7 %first.1.done_ref = f32[2,286,256]{2,1,0:T(8,128)S(1)} custom-call(s32[1]{0:T(128)} %bitcast.6.row_ref, f32[576,256]{1,0:T(8,128)S(1)} %get-tuple-element.15.own_ref, f32[576,256]{1,0:T(8,128)S(1)} %collective-permute-done.3.recv_ref, f32[2,286,256]{2,1,0:T(8,128)S(1)} %get-tuple-element.13.rs_ref, f32[2,286,256]{2,1,0:T(8,128)S(1)} %get-tuple-element.14.ra_ref, ...), custom_call_target="tpu_custom_call" | custom-call | tf_op jit(solution)/shard_map/first/pallas_call | solution.py:188
  55.6 0.0 collective-permute-done.recv_ref
  55.6 2.5 %last.1 = (f32[1144,128]{1,0:T(8,128)}, f32[1144,128]{1,0:T(8,128)}) custom-call(s32[1]{0:T(128)} %bitcast.row_ref, f32[576,256]{1,0:T(8,128)S(1)} %get-tuple-element.10.own_ref, f32[576,256]{1,0:T(8,128)S(1)} %collective-permute-done.recv_ref, f32[2,286,256]{2,1,0:T(8,128)S(1)} %get-tuple-element.13.rs_ref, f32[2,286,256]{2,1,0:T(8,128)S(1)} %get-tuple-element.14.ra_ref, ...), custom_call_target="tpu_custom_call" | custom-call | tf_op jit(solution)/shard_map/last/pallas_call | solution.py:188
Async XLA Ops:
  0.6 1.1 %copy-start.4 = (f32[286,2,2,128]{3,2,1,0:T(2,128)S(1)}, f32[286,2,2,128]{3,2,1,0:T(2,128)}, u32[]{:S(2)}) copy-start(f32[286,2,2,128]{3,2,1,0:T(2,128)} %param.11) | copy-start | bytes 1757188
  1.7 1.1 %copy-start.6 = (f32[286,2,2,128]{3,2,1,0:T(2,128)S(1)}, f32[286,2,2,128]{3,2,1,0:T(2,128)}, u32[]{:S(2)}) copy-start(f32[286,2,2,128]{3,2,1,0:T(2,128)} %param.12) | copy-start | bytes 1757188
  2.8 38.8 %copy-start.5 = (f32[286,2,2,128]{3,2,1,0:T(2,128)S(1)}, f32[286,2,2,128]{3,2,1,0:T(2,128)}, u32[]{:S(2)}) copy-start(f32[286,2,2,128]{3,2,1,0:T(2,128)} %param.11) | copy-start | bytes 1757188
  2.8 38.8 %copy-start.7 = (f32[286,2,2,128]{3,2,1,0:T(2,128)S(1)}, f32[286,2,2,128]{3,2,1,0:T(2,128)}, u32[]{:S(2)}) copy-start(f32[286,2,2,128]{3,2,1,0:T(2,128)} %param.12) | copy-start | bytes 1757188
  4.2 49.7 %collective-permute-start.3 = (f32[576,256]{1,0:T(8,128)S(1)}, f32[576,256]{1,0:T(8,128)S(1)}, u32[]{:S(2)}, u32[]{:S(2)}) collective-permute-start(f32[576,256]{1,0:T(8,128)S(1)} %get-tuple-element.15.own_ref), channel_id=1, source_target_pairs={{0,1},{2,3},{4,5},{6,7},{8,9},{10,11},{12,13},{14,15},{1,0},{3,2},... | collective-permute-start | bytes 1769480 | tf_op jit(solution)/shard_map/ppermute | solution.py:224
  5.0 50.6 %collective-permute-start = (f32[576,256]{1,0:T(8,128)S(1)}, f32[576,256]{1,0:T(8,128)S(1)}, u32[]{:S(2)}, u32[]{:S(2)}) collective-permute-start(f32[576,256]{1,0:T(8,128)S(1)} %get-tuple-element.10.own_ref), channel_id=1, source_target_pairs={{1,2},{3,4},{5,6},{7,8},{9,10},{11,12},{13,14},{2,1},{4,3},{6,5},{... | collective-permute-start | bytes 1769480 | tf_op jit(solution)/shard_map/ppermute | solution.py:223
  11.1 6.9 %collective-permute-start.1 = (f32[286,128]{1,0:T(8,128)}, f32[286,128]{1,0:T(8,128)}, u32[]{:S(2)}, u32[]{:S(2)}) collective-permute-start(f32[286,128]{1,0:T(8,128)} %get-tuple-element.11), channel_id=1, source_target_pairs={{0,16},{32,48},{64,80},{96,112},{128,144},{160,176},{192,208},{224... | collective-permute-start | bytes 439304 | tf_op jit(solution)/shard_map/ppermute | solution.py:225
  11.2 30.4 %collective-permute-start.2 = (f32[286,128]{1,0:T(8,128)}, f32[286,128]{1,0:T(8,128)}, u32[]{:S(2)}, u32[]{:S(2)}) collective-permute-start(f32[286,128]{1,0:T(8,128)} %get-tuple-element.12), channel_id=1, source_target_pairs={{16,32},{48,64},{80,96},{112,128},{144,160},{176,192},{208,224},{3... | collective-permute-start | bytes 439304 | tf_op jit(solution)/shard_map/ppermute | solution.py:226
  41.5 1.3 %copy-start = (f32[3,286,286]{2,1,0:T(8,128)S(1)}, f32[3,286,286]{2,1,0:T(8,128)}, u32[]{:S(2)}) copy-start(f32[3,286,286]{2,1,0:T(8,128)} %up_ref.5) | copy-start | bytes 2944660
  42.9 1.3 %copy-start.2 = (f32[3,286,286]{2,1,0:T(8,128)S(1)}, f32[3,286,286]{2,1,0:T(8,128)}, u32[]{:S(2)}) copy-start(f32[3,286,286]{2,1,0:T(8,128)} %un_ref.5) | copy-start | bytes 2944660
  44.2 1.1 %copy-start.9 = (f32[35,35,35]{2,1,0:T(8,128)S(1)}, f32[35,35,35]{2,1,0:T(8,128)}, u32[]{:S(2)}) copy-start(f32[35,35,35]{2,1,0:T(8,128)} %col_ref.1) | copy-start | bytes 514504
  45.3 0.7 %copy-start.10 = (f32[3,286]{1,0:T(4,128)S(1)}, f32[3,286]{1,0:T(4,128)}, u32[]{:S(2)}) copy-start(f32[3,286]{1,0:T(4,128)} %wt_ref.1) | copy-start | bytes 10300
  46.0 0.7 %copy-start.11 = (s32[2,2,128]{2,1,0:T(2,128)S(1)}, s32[2,2,128]{2,1,0:T(2,128)}, u32[]{:S(2)}) copy-start(s32[2,2,128]{2,1,0:T(2,128)} %param.20) | copy-start | bytes 6148
  46.7 0.7 %copy-start.12 = (s32[2,2,128]{2,1,0:T(2,128)S(1)}, s32[2,2,128]{2,1,0:T(2,128)}, u32[]{:S(2)}) copy-start(s32[2,2,128]{2,1,0:T(2,128)} %param.21) | copy-start | bytes 6148
  47.4 6.5 %copy-start.1 = (f32[3,286,286]{2,1,0:T(8,128)S(1)}, f32[3,286,286]{2,1,0:T(8,128)}, u32[]{:S(2)}) copy-start(f32[3,286,286]{2,1,0:T(8,128)} %up_ref.5) | copy-start | bytes 2944660
  47.4 6.5 %copy-start.3 = (f32[3,286,286]{2,1,0:T(8,128)S(1)}, f32[3,286,286]{2,1,0:T(8,128)}, u32[]{:S(2)}) copy-start(f32[3,286,286]{2,1,0:T(8,128)} %un_ref.5) | copy-start | bytes 2944660
  47.4 6.5 %copy-start.8 = (f32[286,286]{1,0:T(8,128)S(1)}, f32[286,286]{1,0:T(8,128)}, u32[]{:S(2)}) copy-start(f32[286,286]{1,0:T(8,128)} %b_ref.3) | copy-start | bytes 981556

commit v2 on v1

v2 whole, which is shorter than its diff:
```python
import jax
import jax.numpy as jnp
from jax import lax
from jax.experimental import pallas as pl
from jax.experimental.pallas import tpu as pltpu
from jax.sharding import PartitionSpec as P


F32 = jnp.float32
BF16 = jnp.bfloat16
DIRECT = 400


def both_ways(pairs):
    return [(i, j) for i, j in pairs] + [(j, i) for i, j in pairs]


def split(x):
    hi = x.astype(BF16)
    lo = (x - hi.astype(F32)).astype(BF16)
    return hi, lo


def dot(a, b):
    return lax.dot_general(a, b, (((1,), (0,)), ((), ())), preferred_element_type=F32)


def up16(n):
    return (n + 15) // 16 * 16


def dot3(left, b, m):
    high = up16(m)
    both = dot(left, b[0])
    return both[0:m, :] + (both[high : high + m, :] + dot(left[0:m, :], b[1]))


def fetch(pairs, sems):
    copies = [pltpu.make_async_copy(src, dst, sems.at[i]) for i, (src, dst) in enumerate(pairs)]
    for c in copies:
        c.start()
    return copies


def block(ref, z, y):
    return ref[pl.ds(2 * z + y, ref.shape[0] // 4, stride=4), :]


def pack_kernel(par_ref, s_hbm, a_hbm, e_ref, n_ref, w_ref, x_ref, s_ref, a_ref, sems):
    m, half = s_ref.shape[0] // 4, e_ref.shape[0] // 2
    direct = n_ref.shape[0]
    py = par_ref[0] & 1
    copies = fetch([(s_hbm, s_ref), (a_hbm, a_ref)], sems)
    lanes = lax.broadcasted_iota(jnp.int32, (m, 128), 1)
    ends = jnp.zeros((m, 128), F32)
    for f, ref in enumerate((s_ref, a_ref)):
        copies[f].wait()
        for z in range(2):
            cells = pl.ds(z * 128, 128)
            rows = [block(ref, z, y) for y in range(2)]
            e_ref[pl.ds(f * half, m), cells] = jnp.where(py == 0, rows[1], rows[0])
            other = jnp.where(py == 0, rows[0], rows[1])
            near = min(m, direct - f * half)
            n_ref[pl.ds(f * half, near), cells] = other[0:near]
            if near < m:
                w_ref[0 : m - near, cells] = other[near:]
            for y in range(2):
                j = f * 4 + 2 * z + y
                ends = jnp.where((lanes >> 1) == j, pltpu.roll(rows[y], 2 * j + 1, 1), ends)
    x_ref[...] = ends


def interior_kernel(
    par_ref, s_hbm, a_hbm, up_hbm, un_hbm, b_hbm, col_hbm, relax_ref, wt_hbm, dw_ref, codes_hbm, mask_hbm, xe_ref,
    rs_ref, ra_ref, wy_ref, wx_ref, binv_ref,
    s_ref, a_ref, up_ref, un_ref, b_ref, col_ref, wt_ref, codes_ref, mask_ref,
    tab_ref, gain_ref, left_ref, lrem_ref, rrem_ref, lcol_ref, u_ref, sems,
):
    m = rs_ref.shape[1]
    high = up16(m)
    low = col_ref.shape[0]
    step = (low + 7) // 8 * 8
    px = (par_ref[0] >> 1) & 1
    copies = fetch(
        [(s_hbm, s_ref), (a_hbm, a_ref), (col_hbm, col_ref), (codes_hbm, codes_ref), (mask_hbm, mask_ref),
         (wt_hbm, wt_ref), (up_hbm, up_ref), (un_hbm, un_ref), (b_hbm, b_ref)],
        sems,
    )
    lanes = lax.broadcasted_iota(jnp.int32, (m, 128), 1)

    def wide(blocks):
        return jnp.concatenate(blocks, axis=1)

    tab_ref[...] = jnp.zeros_like(tab_ref)
    lrem_ref[...] = jnp.zeros_like(lrem_ref)
    rrem_ref[...] = jnp.zeros_like(rrem_ref)
    for c in copies:
        c.wait()

    tab_ref[0, :] = relax_ref[...]
    tab_ref[1:4, :] = wt_ref[...]
    tab_ref[4, :] = dw_ref[...]
    table = tab_ref[...].T
    thi, tlo = split(table)
    sub = lax.broadcasted_iota(jnp.int32, (8, 128), 0)

    def picked(where_row):
        pick = wide([jnp.where(w, 1.0, 0.0) for w in where_row]).astype(BF16)
        return dot(thi, pick) + dot(tlo, pick)

    def damp_of(y):
        codes = [codes_ref[2 * z + y : 2 * z + y + 1, :] for z in range(2)]
        return picked([(sub == 0) | ((sub > 0) & (sub < 4) & (c == sub)) for c in codes])

    def source_of(y):
        walls = [mask_ref[2 * z + y : 2 * z + y + 1, :] for z in range(2)]
        return picked([(sub == 4) & (w != 0) for w in walls])

    def low_of(ref):
        return wide([ref[pl.ds(2 * z + y, low, stride=4), :] for y in range(2) for z in range(2)])

    s_low, a_low = low_of(s_ref), low_of(a_ref)
    s_hi = s_low.astype(BF16).astype(F32)
    s_lo = (s_low - s_hi).astype(BF16).astype(F32)
    gap = jnp.zeros((step - low, 512), F32)
    right = jnp.concatenate([s_hi, gap, s_lo, gap, s_hi, gap, jnp.zeros((128 - 3 * step, 512), F32)], axis=0).astype(BF16)
    lcol_ref[...] = jnp.zeros_like(lcol_ref)
    for k in range(low):
        c = col_ref[k]
        c = c + c.T
        c_hi = c.astype(BF16).astype(F32)
        at = pl.ds(k * step, low)
        lcol_ref[at, 0:low] = c_hi
        lcol_ref[at, step : step + low] = c_hi
        lcol_ref[at, 2 * step : 2 * step + low] = (c - c_hi).astype(BF16).astype(F32)
    u_ref[...] = dot(lcol_ref[...].astype(BF16), right)
    adgain = jnp.zeros((low, 512), F32)
    for k in range(low):
        u = u_ref[pl.ds(k * step, low), :]
        adgain = adgain + a_low[k : k + 1, :] * u
        gain_ref[k : k + 1, :] = 0.5 * jnp.sum(s_low * u, axis=0, keepdims=True)
    gain = gain_ref[...]

    inverse = b_ref[...]
    for f in range(2):
        mats = [up_ref[0], un_ref[0], up_ref[2] - un_ref[2], up_ref[1], un_ref[1]]
        if f == 1:
            mats = [x.T for x in mats]
        for i, x in enumerate(mats):
            hi, lo = split(x)
            left_ref[5 * f + i, 0:m, :] = hi
            left_ref[5 * f + i, high : high + m, :] = lo
            lrem_ref[2 * f, 0:m, 32 * i : 32 * i + m - 256] = hi[:, 256:].astype(F32)
            lrem_ref[2 * f, high : high + m, 32 * i : 32 * i + m - 256] = lo[:, 256:].astype(F32)
        hi, lo = split(inverse if f == 0 else inverse.T)
        binv_ref[f, 0:m, :] = hi
        binv_ref[f, high : high + m, :] = lo
        wy_ref[2 * f] = left_ref[5 * f + (3 if f == 0 else 4)]
        wy_ref[2 * f + 1] = left_ref[5 * f + (4 if f == 0 else 3)]
        wx_ref[f] = jnp.where(px == 0, left_ref[5 * f + f], left_ref[5 * f + 1 - f])

    ends = xe_ref[...]
    ends = jnp.where(px == 0, ends, pltpu.roll(ends, 2, 1))
    for f, (ref, out_ref) in enumerate(((s_ref, rs_ref), (a_ref, ra_ref))):
        sign = 1.0 if f == 0 else -1.0
        blk = [[block(ref, z, y) for z in range(2)] for y in range(2)]
        step_y = wide([sign * (blk[1][z] - blk[0][z]) for z in range(2)])
        for y in range(2):
            bs, hs = [], []
            for z in range(2):
                j = f * 4 + 2 * z + y
                b = blk[y][z]
                end = pltpu.roll(ends, 126 - 2 * j, 1)
                xm = jnp.where(lanes == 0, jnp.where(px == 1, end, 0.0), pltpu.roll(b, 1, 1))
                xp = jnp.where(lanes == 127, jnp.where(px == 0, end, 0.0), pltpu.roll(b, 127, 1))
                bs.append(sign * (b - xm))
                hs.append(sign * (xp - b))
            behind, ahead = wide(bs), wide(hs)
            dz = blk[y][0] - blk[y][1]
            rights = [behind if f == 0 else ahead, ahead if f == 0 else behind, wide([dz, -dz]), step_y]
            use = 4 if (y == 0) == (f == 0) else 3
            total = None
            for i, r in enumerate(rights):
                k = use if i == 3 else i
                part = dot3(left_ref[5 * f + k, :, 0:256], split(r[0:256]), m)
                total = part if total is None else total + part
                rrem_ref[32 * k : 32 * k + m - 256, :] = r[256:m]
            if use == 4:
                rrem_ref[32 * 3 : 32 * 4, :] = jnp.zeros((32, 256), F32)
            else:
                rrem_ref[32 * 4 : 32 * 5, :] = jnp.zeros((32, 256), F32)
            total = total + dot3(lrem_ref[2 * f].astype(BF16), split(rrem_ref[...]), m)
            res = total + damp_of(y) * wide(blk[y])
            if f == 1:
                res = res - source_of(y)
            out_ref[y] = res
            g = gain if f == 0 else adgain
            out_ref[y, 0:low, :] = out_ref[y, 0:low, :] - g[:, y * 256 : (y + 1) * 256]


def finish(row, own, recv, res, wy_ref, binv_ref):
    m = own[0].shape[0]
    sign = jnp.where(row == 1, 1.0, -1.0).astype(F32)
    new = []
    for f in range(2):
        gap = (recv[f] - own[f]) * (sign if f == 0 else -sign)
        total = res[f] + dot3(wy_ref[2 * f + row], split(gap), m)
        new.append(own[f] - 0.5 * dot3(binv_ref[f], split(total), m))
    return new


def first_kernel(par_ref, own_ref, recv_ref, xo_ref, rs_ref, ra_ref, wy_ref, wx_ref, binv_ref, out_ref, res_ref):
    m, half = rs_ref.shape[1], own_ref.shape[0] // 2
    high = up16(m)
    py, px = par_ref[0] & 1, (par_ref[0] >> 1) & 1
    row = 1 - py
    hi, lo = split(xo_ref[...])
    cols = (hi.astype(F32) + pltpu.roll(lo.astype(F32), 16, 1)).astype(BF16)
    lanes = lax.broadcasted_iota(jnp.int32, (m, 128), 1)
    edge = lanes == jnp.where(px == 0, 0, 127)
    res = []
    for f in range(2):
        both = dot(wx_ref[f], cols)
        fix = both[0:m] + (pltpu.roll(both[0:m], 112, 1) + both[high : high + m])
        fix = jnp.where(px == 0, pltpu.roll(fix, 2, 1), fix) * jnp.where((px == 0) == (f == 0), -1.0, 1.0).astype(F32)
        ref = rs_ref if f == 0 else ra_ref
        parts = []
        for r in range(2):
            at = row if r == 0 else py
            per_z = []
            for z in range(2):
                j0 = f * 4 + 2 * z
                fixes = [pltpu.roll(fix, 126 - 2 * (j0 + y), 1) for y in range(2)]
                add = jnp.where(edge, jnp.where(at == 0, fixes[0], fixes[1]), 0.0)
                per_z.append(ref[at, :, z * 128 : (z + 1) * 128] + add)
            parts.append(jnp.concatenate(per_z, axis=1))
        res.append(parts[0])
        res_ref[f] = parts[1]
    own = [own_ref[0:m, :], own_ref[half : half + m, :]]
    recv = [recv_ref[0:m, :], recv_ref[half : half + m, :]]
    new = finish(row, own, recv, res, wy_ref, binv_ref)
    out_ref[0], out_ref[1] = new


def last_kernel(
    par_ref, n_ref, w_ref, recv_n_ref, recv_w_ref, recv_z_ref, res_ref, wy_ref, binv_ref, done_ref, s_ref, a_ref,
    own_ref, recv_ref,
):
    m, half = res_ref.shape[1], own_ref.shape[0] // 2
    row, outer = par_ref[0] & 1, par_ref[0] >> 2
    direct = n_ref.shape[0]
    own_ref[0:direct, :] = n_ref[...]
    own_ref[direct:, :] = w_ref[...]
    recv_ref[0:direct, :] = recv_n_ref[...]
    recv_ref[direct:, :] = jnp.where(outer == 1, recv_z_ref[...], recv_w_ref[...])
    own = [own_ref[0:m, :], own_ref[half : half + m, :]]
    recv = [recv_ref[0:m, :], recv_ref[half : half + m, :]]
    new = finish(row, own, recv, [res_ref[0], res_ref[1]], wy_ref, binv_ref)
    for f, ref in enumerate((s_ref, a_ref)):
        for z in range(2):
            here = new[f][:, z * 128 : (z + 1) * 128]
            there = done_ref[f, :, z * 128 : (z + 1) * 128]
            ref[pl.ds(2 * z, m, stride=4), :] = jnp.where(row == 0, here, there)
            ref[pl.ds(2 * z + 1, m, stride=4), :] = jnp.where(row == 0, there, here)


def whole(shape):
    return pl.BlockSpec(shape, lambda *_: (0,) * len(shape))


IN_HBM = pl.BlockSpec(memory_space=pltpu.HBM)


def call(kernel, scalars, args, outs, scratch=(), hbm=(), us=1.0):
    in_specs = [IN_HBM if i in hbm else whole(x.shape) for i, x in enumerate(args)]
    args = [pltpu.with_memory_space_constraint(x, pltpu.HBM) if i in hbm else x for i, x in enumerate(args)]
    return pl.pallas_call(
        kernel,
        out_shape=outs,
        grid_spec=pltpu.PrefetchScalarGridSpec(
            num_scalar_prefetch=1,
            grid=(1,),
            in_specs=in_specs,
            out_specs=jax.tree.map(lambda o: whole(o.shape), outs),
            scratch_shapes=list(scratch),
        ),
        compiler_params=pltpu.CompilerParams(vmem_limit_bytes=36 * 1024 * 1024),
        cost_estimate=pl.CostEstimate(flops=int(us * 5e8), bytes_accessed=int(us * 1e6), transcendentals=0),
    )(scalars, *args)


def on_device(
    state, adjoint, upwind_pos, upwind_neg, collision, relax, wall_table, drag_weights, block_inverse,
    cell_codes, wall_mask,
):
    m, low = state.shape[0], collision.shape[0]
    half = (m + 7) // 8 * 8
    high, step = up16(m), half // 8 * 0 + (low + 7) // 8 * 8
    gy, gx = lax.axis_index("gy"), lax.axis_index("gx")
    ny, nx = lax.axis_size("gy"), lax.axis_size("gx")
    px = gx & 1
    spot = gy & 3
    outer = 1 - ((spot ^ (spot >> 1)) & 1)
    par = ((gy & 1) + 2 * px + 4 * outer).astype(jnp.int32).reshape(1)
    s = state.reshape(m * 4, 128)
    a = adjoint.reshape(m * 4, 128)
    sds = jax.ShapeDtypeStruct
    rowbuf = sds((2, m, 256), F32)
    relayed = 2 * half - DIRECT
    own_e, own_n, own_w, ends = call(
        pack_kernel, par, (s, a),
        (sds((2 * half, 256), F32), sds((DIRECT, 256), F32), sds((relayed, 256), F32), sds((m, 128), F32)),
        (pltpu.VMEM(s.shape, F32), pltpu.VMEM(s.shape, F32), pltpu.SemaphoreType.DMA((2,))),
        hbm=(0, 1),
    )
    even = lambda n: both_ways([(i, i + 1) for i in range(0, n - 1, 2)])
    odd = lambda n: both_ways([(i, i + 1) for i in range(1, n - 1, 2)])
    quads = range(0, ny, 4)
    around = both_ways([(q, q + 3) for q in quads] + [(q + 1, q + 2) for q in quads])
    onward = [(q, q + 4) for q in quads if q + 4 < ny] + [(q + 7, q + 3) for q in quads if q + 4 < ny]
    recv_n = lax.ppermute(own_n, "gy", odd(ny))
    recv_w = lax.ppermute(own_w, "gy", around)
    recv_e = lax.ppermute(own_e, "gy", even(ny))
    recv_xe = lax.ppermute(ends, "gx", even(nx))
    recv_xo = lax.ppermute(ends, "gx", odd(nx))
    recv_z = lax.ppermute(recv_w, "gy", onward)
    args = (
        s, a, upwind_pos, upwind_neg, block_inverse, collision, relax, wall_table,
        drag_weights, cell_codes.reshape(4, 128), wall_mask.reshape(4, 128), recv_xe,
    )
    hbm = (0, 1, 2, 3, 4, 5, 7, 9, 10)
    weights = lambda n: sds((n, 2 * high, m), BF16)
    res_s, res_a, wy, wx, binv = call(
        interior_kernel, par, args,
        (rowbuf, rowbuf, weights(4), weights(2), weights(2)),
        tuple(pltpu.VMEM(args[i].shape, args[i].dtype) for i in hbm)
        + (
            pltpu.VMEM((8, m), F32), pltpu.VMEM((low, 512), F32), pltpu.VMEM((10, 2 * high, m), BF16),
            pltpu.VMEM((3, 2 * high, 160), F32), pltpu.VMEM((160, 256), F32), pltpu.VMEM((low * step, 128), F32),
            pltpu.VMEM((low * step, 512), F32), pltpu.SemaphoreType.DMA((9,)),
        ),
        hbm=hbm, us=5.0,
    )
    done, res_o = call(first_kernel, par, (own_e, recv_e, recv_xo, res_s, res_a, wy, wx, binv), (rowbuf, rowbuf))
    out = sds(s.shape, F32)
    s_next, a_next = call(
        last_kernel, par,
        (own_n, own_w, recv_n, recv_w, recv_z, res_o, wy, binv, done), (out, out),
        (pltpu.VMEM((2 * half, 256), F32), pltpu.VMEM((2 * half, 256), F32)),
    )
    return s_next.reshape(state.shape), a_next.reshape(adjoint.shape)


def solution(mesh):
    field, cells = P(None, None, "gy", "gx"), P(None, "gy", "gx")
    in_specs = (field, field, P(), P(), P(), P(), P(), P(), P(), cells, cells)
    return jax.shard_map(
        on_device, mesh=mesh, in_specs=in_specs, out_specs=(field, field), check_vma=False
    )
```

time: 58.6 us -> 39.5 us (0.67)
  waiting for transfers between devices: 23.5 us -> 8.98 us
  local copies, waits for them, and re-layouts: 9.31 us -> 0.01 us
  starting transfers between devices: 12.4 us -> 16.2 us
  Pallas kernels: 12.1 us -> 13.4 us
    ppermute x3 -> x5, waiting for transfers between devices: 23.5 us -> 8.98 us  [the longest x1 8.97 us: on_device(): recv_xo = lax.ppermute(ends, 'gx', odd(nx))]
    unnamed x26 -> x4, local copies, waits for them, and re-layouts: 7.94 us -> 0.01 us
    ppermute x3 -> x5, starting transfers between devices: 11.6 us -> 15.3 us  [the longest x1 7.01 us: on_device(): recv_n = lax.ppermute(own_n, 'gy', odd(ny))]
    reshape x2 -> x0, local copies, waits for them, and re-layouts: 1.37 us -> none  [the longest x1 0.69 us: on_device(): relax.reshape(1, m)]
    pallas_call x4, Pallas kernels: 12.1 us -> 13.4 us  [call(): pl.pallas_call(kernel, out_shape=outs, grid_spec=pltpu.PrefetchScalarGrid...]
  transfers between devices with their start and end apart: 4 -> 6, of which waited for: 1 -> 1; matrix products, arithmetic and copies ran while one was open for 2% -> 0% of each run, Pallas kernels for 14% -> 24%
where the time goes in v2:
time: 39.5 us; the launch traced here: 39.3 us
  starting transfers between devices  16.2 us (41%)
  Pallas kernels  13.4 us (34%)
  waiting for transfers between devices  8.98 us (23%)
  between operations  0.75 us (2%)
    pallas_call x4, Pallas kernels, call(): pl.pallas_call(kernel, out_shape=outs, grid_spec=pltpu.PrefetchScalarGrid...  13.4 us
    ppermute x1, waiting for transfers between devices, on_device(): recv_xo = lax.ppermute(ends, 'gx', odd(nx))  8.97 us
    ppermute x1, starting transfers between devices, on_device(): recv_n = lax.ppermute(own_n, 'gy', odd(ny))  7.01 us
    ppermute x1, starting transfers between devices, on_device(): recv_xo = lax.ppermute(ends, 'gx', odd(nx))  5.2 us
    ppermute x1, starting transfers between devices, on_device(): recv_z = lax.ppermute(recv_w, 'gy', onward)  1.92 us
    ppermute x1, starting transfers between devices, on_device(): recv_w = lax.ppermute(own_w, 'gy', around)  1.14 us
    ppermute x1, starting transfers between devices, on_device(): recv_e = lax.ppermute(own_e, 'gy', even(ny))  0.91 us
  transfers between devices with their start and end apart: 6, of which 1 were waited for; matrix products, arithmetic and copies ran while one was open for 0% of the time, Pallas kernels for 24%

profile of v2, /device:TPU:102, one launch (start us, length us, event | category | flops | bytes accessed | tf_op | source)
XLA Modules:
  0.0 39.3 jit_solution(1205859502081474697)
XLA Ops:
  0.6 0.0 copy-start
  0.6 0.0 copy-start.1
  0.7 1.5 %shard_map.122 = (f32[576,256]{1,0:T(8,128)S(1)}, f32[400,256]{1,0:T(8,128)S(1)}, f32[176,256]{1,0:T(8,128)S(1)}, f32[286,128]{1,0:T(8,128)S(1)}) custom-call(s32[1]{0:T(128)} %bitcast.par_ref, f32[1144,128]{1,0:T(8,128)} %bitcast.7, f32[1144,128]{1,0:T(8,128)} %bitcast.9), custom_call_target="tpu_custom_call" | custom-call | flops 500000000 | bytes 1000000 | tf_op jit(solution)/shard_map/pallas_call | solution.py:277
  2.2 0.9 %collective-permute-start.3 = (f32[576,256]{1,0:T(8,128)S(1)}, f32[576,256]{1,0:T(8,128)S(1)}, u32[]{:S(2)}, u32[]{:S(2)}) collective-permute-start(f32[576,256]{1,0:T(8,128)S(1)} %get-tuple-element.17.own_ref), channel_id=1, source_target_pairs={{0,1},{2,3},{4,5},{6,7},{8,9},{10,11},{12,13},{14,15},{1,0},{3,2},... | collective-permute-start | bytes 1769480 | tf_op jit(solution)/shard_map/ppermute | solution.py:323
  3.1 1.1 %collective-permute-start.1 = (f32[176,256]{1,0:T(8,128)S(1)}, f32[176,256]{1,0:T(8,128)S(1)}, u32[]{:S(2)}, u32[]{:S(2)}) collective-permute-start(f32[176,256]{1,0:T(8,128)S(1)} %get-tuple-element.16.w_ref), channel_id=1, source_target_pairs={{0,3},{4,7},{8,11},{12,15},{1,2},{5,6},{9,10},{13,14},{3,0},{7,4},... | collective-permute-start | bytes 540680 | tf_op jit(solution)/shard_map/ppermute | solution.py:322
  4.3 0.0 collective-permute-start.5
  4.3 7.0 %collective-permute-start = (f32[400,256]{1,0:T(8,128)S(1)}, f32[400,256]{1,0:T(8,128)S(1)}, u32[]{:S(2)}, u32[]{:S(2)}) collective-permute-start(f32[400,256]{1,0:T(8,128)S(1)} %get-tuple-element.15.n_ref), channel_id=1, source_target_pairs={{1,2},{3,4},{5,6},{7,8},{9,10},{11,12},{13,14},{2,1},{4,3},{6,5},{... | collective-permute-start | bytes 1228808 | tf_op jit(solution)/shard_map/ppermute | solution.py:321
  11.3 5.2 %collective-permute-start.4 = (f32[286,128]{1,0:T(8,128)S(1)}, f32[286,128]{1,0:T(8,128)S(1)}, u32[]{:S(2)}, u32[]{:S(2)}) collective-permute-start(f32[286,128]{1,0:T(8,128)S(1)} %get-tuple-element.18), channel_id=1, source_target_pairs={{16,32},{48,64},{80,96},{112,128},{144,160},{176,192},{208,224},{3... | collective-permute-start | bytes 439304 | tf_op jit(solution)/shard_map/ppermute | solution.py:325
  16.5 0.0 collective-permute-done.1.recv_w_ref
  16.5 1.9 %collective-permute-start.2 = (f32[176,256]{1,0:T(8,128)S(1)}, f32[176,256]{1,0:T(8,128)S(1)}, u32[]{:S(2)}, u32[]{:S(2)}) collective-permute-start(f32[176,256]{1,0:T(8,128)S(1)} %collective-permute-done.1.recv_w_ref), channel_id=1, source_target_pairs={{0,4},{4,8},{8,12},{7,3},{11,7},{15,11},{16,20},{20,24},{24,28},{2... | collective-permute-start | bytes 540680 | tf_op jit(solution)/shard_map/ppermute | solution.py:326
  18.4 0.0 collective-permute-done.5.xe_ref
  18.4 0.0 copy-done
  18.4 0.0 copy-done.1
  18.5 7.4 %shard_map.123 = (f32[2,286,256]{2,1,0:T(8,128)S(1)}, f32[2,286,256]{2,1,0:T(8,128)S(1)}, bf16[4,576,286]{2,1,0:T(8,128)(2,1)S(1)}, bf16[2,576,286]{2,1,0:T(8,128)(2,1)S(1)}, bf16[2,576,286]{2,1,0:T(8,128)(2,1)S(1)}) custom-call(s32[1]{0:T(128)} %bitcast.par_ref, f32[1144,128]{1,0:T(8,128)} %bitcast.8, f32[1144,128]{1,0:T(8,128)} %bitcast.10, ...), custom_call_target="tpu_custom_call" | custom-call | flops 2500000000 | bytes 5000000 | tf_op jit(solution)/shard_map/pallas_call | solution.py:277
  25.9 9.0 %collective-permute-done.4.xo_ref = f32[286,128]{1,0:T(8,128)S(1)} collective-permute-done((f32[286,128]{1,0:T(8,128)S(1)}, f32[286,128]{1,0:T(8,128)S(1)}, u32[]{:S(2)}, u32[]{:S(2)}) %collective-permute-start.4) | collective-permute-done | bytes 146464 | tf_op jit(solution)/shard_map/ppermute | solution.py:325
  34.9 0.0 collective-permute-done.3.recv_ref
  34.9 1.9 %shard_map.124 = (f32[2,286,256]{2,1,0:T(8,128)S(1)}, f32[2,286,256]{2,1,0:T(8,128)S(1)}) custom-call(s32[1]{0:T(128)} %bitcast.par_ref, f32[576,256]{1,0:T(8,128)S(1)} %get-tuple-element.17.own_ref, f32[576,256]{1,0:T(8,128)S(1)} %collective-permute-done.3.recv_ref, f32[286,128]{1,0:T(8,128)S(1)} %collective-permute-done.4.xo_ref, ...), custom_call_target="tpu_custom_call" | custom-call | flops 500000000 | bytes 1000000 | tf_op jit(solution)/shard_map/pallas_call | solution.py:277
  36.8 0.0 collective-permute-done.2.recv_z_ref
  36.8 0.0 collective-permute-done.recv_n_ref
  36.9 2.5 %shard_map.125 = (f32[1144,128]{1,0:T(8,128)}, f32[1144,128]{1,0:T(8,128)}) custom-call(s32[1]{0:T(128)} %bitcast.par_ref, f32[400,256]{1,0:T(8,128)S(1)} %get-tuple-element.15.n_ref, f32[176,256]{1,0:T(8,128)S(1)} %get-tuple-element.16.w_ref, f32[400,256]{1,0:T(8,128)S(1)} %collective-permute-done.recv_n_ref, ...), custom_call_target="tpu_custom_call" | custom-call | flops 500000000 | bytes 1000000 | tf_op jit(solution)/shard_map/pallas_call | solution.py:277
Async XLA Ops:
  0.6 17.8 %copy-start = (f32[286]{0:T(512)S(1)}, f32[286]{0:T(512)}, u32[]{:S(2)}) copy-start(f32[286]{0:T(512)} %relax_ref.1) | copy-start | bytes 3436
  0.6 17.8 %copy-start.1 = (f32[286]{0:T(512)S(1)}, f32[286]{0:T(512)}, u32[]{:S(2)}) copy-start(f32[286]{0:T(512)} %dw_ref.1) | copy-start | bytes 3436
  2.2 32.7 %collective-permute-start.3 = (f32[576,256]{1,0:T(8,128)S(1)}, f32[576,256]{1,0:T(8,128)S(1)}, u32[]{:S(2)}, u32[]{:S(2)}) collective-permute-start(f32[576,256]{1,0:T(8,128)S(1)} %get-tuple-element.17.own_ref), channel_id=1, source_target_pairs={{0,1},{2,3},{4,5},{6,7},{8,9},{10,11},{12,13},{14,15},{1,0},{3,2},... | collective-permute-start | bytes 1769480 | tf_op jit(solution)/shard_map/ppermute | solution.py:323
  3.1 13.4 %collective-permute-start.1 = (f32[176,256]{1,0:T(8,128)S(1)}, f32[176,256]{1,0:T(8,128)S(1)}, u32[]{:S(2)}, u32[]{:S(2)}) collective-permute-start(f32[176,256]{1,0:T(8,128)S(1)} %get-tuple-element.16.w_ref), channel_id=1, source_target_pairs={{0,3},{4,7},{8,11},{12,15},{1,2},{5,6},{9,10},{13,14},{3,0},{7,4},... | collective-permute-start | bytes 540680 | tf_op jit(solution)/shard_map/ppermute | solution.py:322
  4.3 14.2 %collective-permute-start.5 = (f32[286,128]{1,0:T(8,128)S(1)}, f32[286,128]{1,0:T(8,128)S(1)}, u32[]{:S(2)}, u32[]{:S(2)}) collective-permute-start(f32[286,128]{1,0:T(8,128)S(1)} %get-tuple-element.18), channel_id=1, source_target_pairs={{0,16},{32,48},{64,80},{96,112},{128,144},{160,176},{192,208},{224... | collective-permute-start | bytes 439304 | tf_op jit(solution)/shard_map/ppermute | solution.py:324
  4.3 32.6 %collective-permute-start = (f32[400,256]{1,0:T(8,128)S(1)}, f32[400,256]{1,0:T(8,128)S(1)}, u32[]{:S(2)}, u32[]{:S(2)}) collective-permute-start(f32[400,256]{1,0:T(8,128)S(1)} %get-tuple-element.15.n_ref), channel_id=1, source_target_pairs={{1,2},{3,4},{5,6},{7,8},{9,10},{11,12},{13,14},{2,1},{4,3},{6,5},{... | collective-permute-start | bytes 1228808 | tf_op jit(solution)/shard_map/ppermute | solution.py:321
  11.3 23.6 %collective-permute-start.4 = (f32[286,128]{1,0:T(8,128)S(1)}, f32[286,128]{1,0:T(8,128)S(1)}, u32[]{:S(2)}, u32[]{:S(2)}) collective-permute-start(f32[286,128]{1,0:T(8,128)S(1)} %get-tuple-element.18), channel_id=1, source_target_pairs={{16,32},{48,64},{80,96},{112,128},{144,160},{176,192},{208,224},{3... | collective-permute-start | bytes 439304 | tf_op jit(solution)/shard_map/ppermute | solution.py:325
  16.5 20.3 %collective-permute-start.2 = (f32[176,256]{1,0:T(8,128)S(1)}, f32[176,256]{1,0:T(8,128)S(1)}, u32[]{:S(2)}, u32[]{:S(2)}) collective-permute-start(f32[176,256]{1,0:T(8,128)S(1)} %collective-permute-done.1.recv_w_ref), channel_id=1, source_target_pairs={{0,4},{4,8},{8,12},{7,3},{11,7},{15,11},{16,20},{20,24},{24,28},{2... | collective-permute-start | bytes 540680 | tf_op jit(solution)/shard_map/ppermute | solution.py:326

commit v3 on v2

--- a/solution.py
+++ b/solution.py
@@ -8,7 +8,7 @@
 
 F32 = jnp.float32
 BF16 = jnp.bfloat16
-DIRECT = 400
+DIRECT = 376
 
 
 def both_ways(pairs):
@@ -68,6 +68,10 @@
                 j = f * 4 + 2 * z + y
                 ends = jnp.where((lanes >> 1) == j, pltpu.roll(rows[y], 2 * j + 1, 1), ends)
     x_ref[...] = ends
+
+
+def merge_kernel(par_ref, own_ref, other_ref, out_ref):
+    out_ref[...] = own_ref[...] + pltpu.roll(other_ref[...], 16, 1)
 
 
 def interior_kernel(
@@ -209,14 +213,16 @@
     return new
 
 
-def first_kernel(par_ref, own_ref, recv_ref, xo_ref, rs_ref, ra_ref, wy_ref, wx_ref, binv_ref, out_ref, res_ref):
+def first_kernel(par_ref, own_ref, recv_ref, xo_ref, xf_ref, rs_ref, ra_ref, wy_ref, wx_ref, binv_ref, out_ref, res_ref):
     m, half = rs_ref.shape[1], own_ref.shape[0] // 2
     high = up16(m)
     py, px = par_ref[0] & 1, (par_ref[0] >> 1) & 1
     row = 1 - py
-    hi, lo = split(xo_ref[...])
+    outer = par_ref[0] >> 2
+    lanes = lax.broadcasted_iota(jnp.int32, (m, 128), 1)
+    came = jnp.where(outer == 1, pltpu.roll(xf_ref[...], 112, 1), xo_ref[...])
+    hi, lo = split(jnp.where(lanes < 16, came, 0.0))
     cols = (hi.astype(F32) + pltpu.roll(lo.astype(F32), 16, 1)).astype(BF16)
-    lanes = lax.broadcasted_iota(jnp.int32, (m, 128), 1)
     edge = lanes == jnp.where(px == 0, 0, 127)
     res = []
     for f in range(2):
@@ -322,7 +328,11 @@
     recv_w = lax.ppermute(own_w, "gy", around)
     recv_e = lax.ppermute(own_e, "gy", even(ny))
     recv_xe = lax.ppermute(ends, "gx", even(nx))
-    recv_xo = lax.ppermute(ends, "gx", odd(nx))
+    ends_p = lax.ppermute(ends, "gy", even(ny))
+    ends_m = call(merge_kernel, par, (ends, ends_p), sds((m, 128), F32))
+    inner = [g for g in range(ny) if g % 4 in (1, 2)]
+    recv_xo = lax.ppermute(ends_m, ("gx", "gy"), [(i * ny + g, j * ny + g) for i, j in odd(nx) for g in inner])
+    recv_xf = lax.ppermute(recv_xo, "gy", even(ny))
     recv_z = lax.ppermute(recv_w, "gy", onward)
     args = (
         s, a, upwind_pos, upwind_neg, block_inverse, collision, relax, wall_table,
@@ -341,7 +351,9 @@
         ),
         hbm=hbm, us=5.0,
     )
-    done, res_o = call(first_kernel, par, (own_e, recv_e, recv_xo, res_s, res_a, wy, wx, binv), (rowbuf, rowbuf))
+    done, res_o = call(
+        first_kernel, par, (own_e, recv_e, recv_xo, recv_xf, res_s, res_a, wy, wx, binv), (rowbuf, rowbuf)
+    )
     out = sds(s.shape, F32)
     s_next, a_next = call(
         last_kernel, par,

time: 39.5 us -> 49.7 us (1.26)
  the two profiles are of different devices: /device:TPU:102 before, /device:TPU:70 now
where the time goes in v3:
time: 49.7 us; the launch traced here: 49.6 us
  waiting for transfers between devices  23.5 us (47%)
  Pallas kernels  13.6 us (27%)
  starting transfers between devices  11.7 us (24%)
  between operations  0.79 us (2%)
    ppermute x1, waiting for transfers between devices, on_device(): ends_p = lax.ppermute(ends, 'gy', even(ny))  15.7 us
    pallas_call x5, Pallas kernels, call(): pl.pallas_call(kernel, out_shape=outs, grid_spec=pltpu.PrefetchScalarGrid...  13.6 us
    ppermute x1, waiting for transfers between devices, on_device(): recv_n = lax.ppermute(own_n, 'gy', odd(ny))  7.74 us
    ppermute x1, starting transfers between devices, on_device(): recv_n = lax.ppermute(own_n, 'gy', odd(ny))  6.31 us
    ppermute x1, starting transfers between devices, on_device(): recv_z = lax.ppermute(recv_w, 'gy', onward)  1.92 us
    ppermute x1, starting transfers between devices, on_device(): ends_p = lax.ppermute(ends, 'gy', even(ny))  1.2 us
  transfers between devices with their start and end apart: 8, of which 2 were waited for; matrix products, arithmetic and copies ran while one was open for 0% of the time, Pallas kernels for 19%

profile of v3, /device:TPU:70, one launch (start us, length us, event | category | flops | bytes accessed | tf_op | source)
XLA Modules:
  0.0 49.6 jit_solution(6446318167522845014)
XLA Ops:
  0.6 1.5 %shard_map.122 = (f32[576,256]{1,0:T(8,128)S(1)}, f32[376,256]{1,0:T(8,128)S(1)}, f32[200,256]{1,0:T(8,128)S(1)}, f32[286,128]{1,0:T(8,128)S(1)}) custom-call(s32[1]{0:T(128)} %bitcast.par_ref, f32[1144,128]{1,0:T(8,128)} %bitcast.7, f32[1144,128]{1,0:T(8,128)} %bitcast.9), custom_call_target="tpu_custom_call" | custom-call | flops 500000000 | bytes 1000000 | tf_op jit(solution)/shard_map/pallas_call | solution.py:283
  2.2 0.0 copy-start
  2.2 0.0 copy-start.1
  2.2 0.9 %collective-permute-start.3 = (f32[576,256]{1,0:T(8,128)S(1)}, f32[576,256]{1,0:T(8,128)S(1)}, u32[]{:S(2)}, u32[]{:S(2)}) collective-permute-start(f32[576,256]{1,0:T(8,128)S(1)} %get-tuple-element.17.own_ref), channel_id=1, source_target_pairs={{0,1},{2,3},{4,5},{6,7},{8,9},{10,11},{12,13},{14,15},{1,0},{3,2},... | collective-permute-start | bytes 1769480 | tf_op jit(solution)/shard_map/ppermute | solution.py:329
  3.1 1.2 %collective-permute-start.4 = (f32[286,128]{1,0:T(8,128)S(1)}, f32[286,128]{1,0:T(8,128)S(1)}, u32[]{:S(2)}, u32[]{:S(2)}) collective-permute-start(f32[286,128]{1,0:T(8,128)S(1)} %get-tuple-element.18.own_ref), channel_id=1, source_target_pairs={{0,1},{2,3},{4,5},{6,7},{8,9},{10,11},{12,13},{14,15},{1,0},{3,2},... | collective-permute-start | bytes 439304 | tf_op jit(solution)/shard_map/ppermute | solution.py:331
  4.3 0.5 collective-permute-start.1
  4.8 15.7 %collective-permute-done.4.other_ref = f32[286,128]{1,0:T(8,128)S(1)} collective-permute-done((f32[286,128]{1,0:T(8,128)S(1)}, f32[286,128]{1,0:T(8,128)S(1)}, u32[]{:S(2)}, u32[]{:S(2)}) %collective-permute-start.4) | collective-permute-done | bytes 146464 | tf_op jit(solution)/shard_map/ppermute | solution.py:331
  20.5 0.1 shard_map.123
  20.6 0.7 %collective-permute-start.5 = (f32[286,128]{1,0:T(8,128)S(1)}, f32[286,128]{1,0:T(8,128)S(1)}, u32[]{:S(2)}, u32[]{:S(2)}) collective-permute-start(f32[286,128]{1,0:T(8,128)S(1)} %shard_map.123), channel_id=1, source_target_pairs={{17,33},{18,34},{21,37},{22,38},{25,41},{26,42},{29,45},{30,46},{4... | collective-permute-start | bytes 439304 | tf_op jit(solution)/shard_map/ppermute | solution.py:334
  21.3 0.1 collective-permute-start.7
  21.4 6.3 %collective-permute-start = (f32[376,256]{1,0:T(8,128)S(1)}, f32[376,256]{1,0:T(8,128)S(1)}, u32[]{:S(2)}, u32[]{:S(2)}) collective-permute-start(f32[376,256]{1,0:T(8,128)S(1)} %get-tuple-element.15.n_ref), channel_id=1, source_target_pairs={{1,2},{3,4},{5,6},{7,8},{9,10},{11,12},{13,14},{2,1},{4,3},{6,5},{... | collective-permute-start | bytes 1155080 | tf_op jit(solution)/shard_map/ppermute | solution.py:327
  27.7 0.0 collective-permute-done.1.recv_w_ref
  27.7 1.9 %collective-permute-start.2 = (f32[200,256]{1,0:T(8,128)S(1)}, f32[200,256]{1,0:T(8,128)S(1)}, u32[]{:S(2)}, u32[]{:S(2)}) collective-permute-start(f32[200,256]{1,0:T(8,128)S(1)} %collective-permute-done.1.recv_w_ref), channel_id=1, source_target_pairs={{0,4},{4,8},{8,12},{7,3},{11,7},{15,11},{16,20},{20,24},{24,28},{2... | collective-permute-start | bytes 614408 | tf_op jit(solution)/shard_map/ppermute | solution.py:336
  29.7 0.0 collective-permute-done.5.xo_ref
  29.7 0.1 collective-permute-start.6
  29.8 0.0 collective-permute-done.7.xe_ref
  29.8 0.0 copy-done
  29.8 0.0 copy-done.1
  29.8 7.4 %shard_map.124 = (f32[2,286,256]{2,1,0:T(8,128)S(1)}, f32[2,286,256]{2,1,0:T(8,128)S(1)}, bf16[4,576,286]{2,1,0:T(8,128)(2,1)S(1)}, bf16[2,576,286]{2,1,0:T(8,128)(2,1)S(1)}, bf16[2,576,286]{2,1,0:T(8,128)(2,1)S(1)}) custom-call(s32[1]{0:T(128)} %bitcast.par_ref, f32[1144,128]{1,0:T(8,128)} %bitcast.8, f32[1144,128]{1,0:T(8,128)} %bitcast.10, ...), custom_call_target="tpu_custom_call" | custom-call | flops 2500000000 | bytes 5000000 | tf_op jit(solution)/shard_map/pallas_call | solution.py:283
  37.2 0.0 collective-permute-done.6.xf_ref
  37.2 0.0 collective-permute-done.3.recv_ref
  37.3 2.1 %shard_map.125 = (f32[2,286,256]{2,1,0:T(8,128)S(1)}, f32[2,286,256]{2,1,0:T(8,128)S(1)}) custom-call(s32[1]{0:T(128)} %bitcast.par_ref, f32[576,256]{1,0:T(8,128)S(1)} %get-tuple-element.17.own_ref, f32[576,256]{1,0:T(8,128)S(1)} %collective-permute-done.3.recv_ref, f32[286,128]{1,0:T(8,128)S(1)} %collective-permute-done.5.xo_ref, ...), custom_call_target="tpu_custom_call" | custom-call | flops 500000000 | bytes 1000000 | tf_op jit(solution)/shard_map/pallas_call | solution.py:283
  39.4 7.7 %collective-permute-done.recv_n_ref = f32[376,256]{1,0:T(8,128)S(1)} collective-permute-done((f32[376,256]{1,0:T(8,128)S(1)}, f32[376,256]{1,0:T(8,128)S(1)}, u32[]{:S(2)}, u32[]{:S(2)}) %collective-permute-start) | collective-permute-done | bytes 385056 | tf_op jit(solution)/shard_map/ppermute | solution.py:327
  47.1 0.0 collective-permute-done.2.recv_z_ref
  47.1 2.5 %shard_map.126 = (f32[1144,128]{1,0:T(8,128)}, f32[1144,128]{1,0:T(8,128)}) custom-call(s32[1]{0:T(128)} %bitcast.par_ref, f32[376,256]{1,0:T(8,128)S(1)} %get-tuple-element.15.n_ref, f32[200,256]{1,0:T(8,128)S(1)} %get-tuple-element.16.w_ref, f32[376,256]{1,0:T(8,128)S(1)} %collective-permute-done.recv_n_ref, ...), custom_call_target="tpu_custom_call" | custom-call | flops 500000000 | bytes 1000000 | tf_op jit(solution)/shard_map/pallas_call | solution.py:283
Async XLA Ops:
  2.2 27.6 %copy-start = (f32[286]{0:T(512)S(1)}, f32[286]{0:T(512)}, u32[]{:S(2)}) copy-start(f32[286]{0:T(512)} %relax_ref.1) | copy-start | bytes 3436
  2.2 27.6 %copy-start.1 = (f32[286]{0:T(512)S(1)}, f32[286]{0:T(512)}, u32[]{:S(2)}) copy-start(f32[286]{0:T(512)} %dw_ref.1) | copy-start | bytes 3436
  2.2 35.1 %collective-permute-start.3 = (f32[576,256]{1,0:T(8,128)S(1)}, f32[576,256]{1,0:T(8,128)S(1)}, u32[]{:S(2)}, u32[]{:S(2)}) collective-permute-start(f32[576,256]{1,0:T(8,128)S(1)} %get-tuple-element.17.own_ref), channel_id=1, source_target_pairs={{0,1},{2,3},{4,5},{6,7},{8,9},{10,11},{12,13},{14,15},{1,0},{3,2},... | collective-permute-start | bytes 1769480 | tf_op jit(solution)/shard_map/ppermute | solution.py:329
  3.1 17.4 %collective-permute-start.4 = (f32[286,128]{1,0:T(8,128)S(1)}, f32[286,128]{1,0:T(8,128)S(1)}, u32[]{:S(2)}, u32[]{:S(2)}) collective-permute-start(f32[286,128]{1,0:T(8,128)S(1)} %get-tuple-element.18.own_ref), channel_id=1, source_target_pairs={{0,1},{2,3},{4,5},{6,7},{8,9},{10,11},{12,13},{14,15},{1,0},{3,2},... | collective-permute-start | bytes 439304 | tf_op jit(solution)/shard_map/ppermute | solution.py:331
  4.3 23.4 %collective-permute-start.1 = (f32[200,256]{1,0:T(8,128)S(1)}, f32[200,256]{1,0:T(8,128)S(1)}, u32[]{:S(2)}, u32[]{:S(2)}) collective-permute-start(f32[200,256]{1,0:T(8,128)S(1)} %get-tuple-element.16.w_ref), channel_id=1, source_target_pairs={{0,3},{4,7},{8,11},{12,15},{1,2},{5,6},{9,10},{13,14},{3,0},{7,4},... | collective-permute-start | bytes 614408 | tf_op jit(solution)/shard_map/ppermute | solution.py:328
  20.6 9.0 %collective-permute-start.5 = (f32[286,128]{1,0:T(8,128)S(1)}, f32[286,128]{1,0:T(8,128)S(1)}, u32[]{:S(2)}, u32[]{:S(2)}) collective-permute-start(f32[286,128]{1,0:T(8,128)S(1)} %shard_map.123), channel_id=1, source_target_pairs={{17,33},{18,34},{21,37},{22,38},{25,41},{26,42},{29,45},{30,46},{4... | collective-permute-start | bytes 439304 | tf_op jit(solution)/shard_map/ppermute | solution.py:334
  21.3 8.5 %collective-permute-start.7 = (f32[286,128]{1,0:T(8,128)S(1)}, f32[286,128]{1,0:T(8,128)S(1)}, u32[]{:S(2)}, u32[]{:S(2)}) collective-permute-start(f32[286,128]{1,0:T(8,128)S(1)} %get-tuple-element.18.own_ref), channel_id=1, source_target_pairs={{0,16},{32,48},{64,80},{96,112},{128,144},{160,176},{192,208},{224... | collective-permute-start | bytes 439304 | tf_op jit(solution)/shard_map/ppermute | solution.py:330
  21.4 25.7 %collective-permute-start = (f32[376,256]{1,0:T(8,128)S(1)}, f32[376,256]{1,0:T(8,128)S(1)}, u32[]{:S(2)}, u32[]{:S(2)}) collective-permute-start(f32[376,256]{1,0:T(8,128)S(1)} %get-tuple-element.15.n_ref), channel_id=1, source_target_pairs={{1,2},{3,4},{5,6},{7,8},{9,10},{11,12},{13,14},{2,1},{4,3},{6,5},{... | collective-permute-start | bytes 1155080 | tf_op jit(solution)/shard_map/ppermute | solution.py:327
  27.7 19.4 %collective-permute-start.2 = (f32[200,256]{1,0:T(8,128)S(1)}, f32[200,256]{1,0:T(8,128)S(1)}, u32[]{:S(2)}, u32[]{:S(2)}) collective-permute-start(f32[200,256]{1,0:T(8,128)S(1)} %collective-permute-done.1.recv_w_ref), channel_id=1, source_target_pairs={{0,4},{4,8},{8,12},{7,3},{11,7},{15,11},{16,20},{20,24},{24,28},{2... | collective-permute-start | bytes 614408 | tf_op jit(solution)/shard_map/ppermute | solution.py:336
  29.7 7.6 %collective-permute-start.6 = (f32[286,128]{1,0:T(8,128)S(1)}, f32[286,128]{1,0:T(8,128)S(1)}, u32[]{:S(2)}, u32[]{:S(2)}) collective-permute-start(f32[286,128]{1,0:T(8,128)S(1)} %collective-permute-done.5.xo_ref), channel_id=1, source_target_pairs={{0,1},{2,3},{4,5},{6,7},{8,9},{10,11},{12,13},{14,15},{1,0},{3,2},... | collective-permute-start | bytes 439304 | tf_op jit(solution)/shard_map/ppermute | solution.py:335

commit v4 on v3

v4 whole, which is shorter than its diff:
```python
import jax
import jax.numpy as jnp
from jax import lax
from jax.experimental import pallas as pl
from jax.experimental.pallas import tpu as pltpu
from jax.sharding import PartitionSpec as P


F32 = jnp.float32
BF16 = jnp.bfloat16
DIRECT = 376


def both_ways(pairs):
    return [(i, j) for i, j in pairs] + [(j, i) for i, j in pairs]


def split(x):
    hi = x.astype(BF16)
    lo = (x - hi.astype(F32)).astype(BF16)
    return hi, lo


def dot(a, b):
    return lax.dot_general(a, b, (((1,), (0,)), ((), ())), preferred_element_type=F32)


def up16(n):
    return (n + 15) // 16 * 16


def dot3(left, b, m):
    high = up16(m)
    both = dot(left, b[0])
    return both[0:m, :] + (both[high : high + m, :] + dot(left[0:m, :], b[1]))


def fetch(pairs, sems):
    copies = [pltpu.make_async_copy(src, dst, sems.at[i]) for i, (src, dst) in enumerate(pairs)]
    for c in copies:
        c.start()
    return copies


def block(ref, z, y):
    return ref[pl.ds(2 * z + y, ref.shape[0] // 4, stride=4), :]


def fold(x, rows):
    return sum(pltpu.roll(x[g * rows : (g + 1) * rows], 32 * g, 1) if g else x[0:rows] for g in range(4))


def unfold(x, m):
    groups = [pltpu.roll(x, 128 - 32 * g, 1) if g else x for g in range(4)]
    return jnp.concatenate(groups, axis=0)[0:m]


def pack_kernel(par_ref, s_hbm, a_hbm, e_ref, n_ref, w_ref, x_ref, s_ref, a_ref, sems):
    m, half = s_ref.shape[0] // 4, e_ref.shape[0] // 2
    direct = n_ref.shape[0]
    py = par_ref[0] & 1
    copies = fetch([(s_hbm, s_ref), (a_hbm, a_ref)], sems)
    lanes = lax.broadcasted_iota(jnp.int32, (m, 128), 1)
    ends = jnp.zeros((m, 128), F32)
    for f, ref in enumerate((s_ref, a_ref)):
        copies[f].wait()
        for z in range(2):
            cells = pl.ds(z * 128, 128)
            rows = [block(ref, z, y) for y in range(2)]
            e_ref[pl.ds(f * half, m), cells] = jnp.where(py == 0, rows[1], rows[0])
            other = jnp.where(py == 0, rows[0], rows[1])
            near = min(m, direct - f * half)
            n_ref[pl.ds(f * half, near), cells] = other[0:near]
            if near < m:
                w_ref[0 : m - near, cells] = other[near:]
            for y in range(2):
                j = f * 4 + 2 * z + y
                ends = jnp.where((lanes >> 1) == j, pltpu.roll(rows[y], 2 * j + 1, 1), ends)
    rows = x_ref.shape[0]
    x_ref[...] = fold(jnp.concatenate([ends, jnp.zeros((4 * rows - m, 128), F32)], axis=0), rows)


def merge_kernel(par_ref, own_ref, other_ref, out_ref):
    out_ref[...] = own_ref[...] + pltpu.roll(other_ref[...], 16, 1)


def prep_kernel(
    par_ref, s_hbm, a_hbm, up_ref, un_ref, b_hbm, col_ref,
    s_ref, a_ref, left_ref, lrem_ref, binv_ref, comp_ref, lcol_ref,
    b_ref, rem_ref, cmat_ref, sems,
):
    m = b_ref.shape[0]
    high = up16(m)
    low = col_ref.shape[0]
    step = (low + 7) // 8 * 8
    row = par_ref[0] & 1
    copies = fetch(
        [(b_hbm, b_ref), (s_hbm, s_ref), (a_hbm, a_ref)], sems
    )
    rem_ref[...] = jnp.zeros_like(rem_ref)
    cmat_ref[...] = jnp.zeros_like(cmat_ref)
    meets = []
    for f in range(2):
        mats = [up_ref[0], un_ref[0], up_ref[2] - un_ref[2], up_ref[1], un_ref[1]]
        if f == 1:
            mats = [x.T for x in mats]
        for i, x in enumerate(mats):
            hi, lo = split(x)
            left_ref[5 * f + i, 0:m, :] = hi
            left_ref[5 * f + i, high : high + m, :] = lo
            rem_ref[f, 0:m, 32 * i : 32 * i + m - 256] = hi[:, 256:].astype(F32)
            rem_ref[f, high : high + m, 32 * i : 32 * i + m - 256] = lo[:, 256:].astype(F32)
        lrem_ref[f] = rem_ref[f].astype(BF16)
        meets.append(jnp.where((row == 0) == (f == 0), mats[3], mats[4]))
    copies[0].wait()
    for f in range(2):
        hi, lo = split(b_ref[...] if f == 0 else b_ref[...].T)
        binv_ref[f, 0:m, :] = hi
        binv_ref[f, high : high + m, :] = lo
        scale = jnp.where((row == 1) == (f == 0), -0.5, 0.5).astype(F32)
        hi, lo = split(scale * dot3(binv_ref[f], split(meets[f]), m))
        comp_ref[f, 0:m, :] = hi
        comp_ref[f, high : high + m, :] = lo
    for k in range(low):
        c = col_ref[k]
        c = c + c.T
        c_hi = c.astype(BF16).astype(F32)
        at = pl.ds(k * step, low)
        cmat_ref[at, 0:low] = c_hi
        cmat_ref[at, step : step + low] = c_hi
        cmat_ref[at, 2 * step : 2 * step + low] = (c - c_hi).astype(BF16).astype(F32)
    lcol_ref[...] = cmat_ref[...].astype(BF16)
    copies[1].wait()
    copies[2].wait()


def interior_kernel(
    par_ref, s_ref, a_ref, left_ref, lrem_ref, lcol_ref, relax_ref, wt_hbm, dw_ref, codes_hbm, mask_hbm, xe_ref,
    rs_ref, ra_ref, wt_ref, codes_ref, mask_ref, tab_ref, gain_ref, rrem_ref, u_ref, sems,
):
    m = rs_ref.shape[1]
    low = gain_ref.shape[0]
    step = (low + 7) // 8 * 8
    px = (par_ref[0] >> 1) & 1
    copies = fetch([(codes_hbm, codes_ref), (mask_hbm, mask_ref), (wt_hbm, wt_ref)], sems)
    lanes = lax.broadcasted_iota(jnp.int32, (m, 128), 1)

    def wide(blocks):
        return jnp.concatenate(blocks, axis=1)

    tab_ref[...] = jnp.zeros_like(tab_ref)
    rrem_ref[...] = jnp.zeros_like(rrem_ref)

    def low_of(ref):
        return wide([ref[pl.ds(2 * z + y, low, stride=4), :] for y in range(2) for z in range(2)])

    s_low, a_low = low_of(s_ref), low_of(a_ref)
    s_hi = s_low.astype(BF16).astype(F32)
    s_lo = (s_low - s_hi).astype(BF16).astype(F32)
    gap = jnp.zeros((step - low, 512), F32)
    right = jnp.concatenate([s_hi, gap, s_lo, gap, s_hi, gap, jnp.zeros((128 - 3 * step, 512), F32)], axis=0).astype(BF16)
    u_ref[...] = dot(lcol_ref[...], right)
    adgain = jnp.zeros((low, 512), F32)
    for k in range(low):
        u = u_ref[pl.ds(k * step, low), :]
        adgain = adgain + a_low[k : k + 1, :] * u
        gain_ref[k : k + 1, :] = 0.5 * jnp.sum(s_low * u, axis=0, keepdims=True)
    gain = gain_ref[...]

    for c in copies:
        c.wait()
    tab_ref[0, :] = relax_ref[...]
    tab_ref[1:4, :] = wt_ref[...]
    tab_ref[4, :] = dw_ref[...]
    tab_hi = tab_ref[0:8, :].astype(BF16).astype(F32)
    tab_ref[8:16, :] = tab_ref[0:8, :] - tab_hi
    tab_ref[0:8, :] = tab_hi
    table = tab_ref[...].T.astype(BF16)
    sub = lax.broadcasted_iota(jnp.int32, (16, 128), 0) & 7

    def picked(where_row):
        return dot(table, wide([jnp.where(w, 1.0, 0.0) for w in where_row]).astype(BF16))

    codes = [codes_ref[q : q + 1, :] for q in range(4)]
    walls = [mask_ref[q : q + 1, :] for q in range(4)]
    damp = [
        picked([(sub == 0) | ((sub > 0) & (sub < 4) & (codes[2 * z + y] == sub)) for z in range(2)]) for y in range(2)
    ]
    source = [picked([(sub == 4) & (walls[2 * z + y] != 0) for z in range(2)]) for y in range(2)]

    ends = unfold(xe_ref[...], m)
    ends = jnp.where(px == 0, ends, pltpu.roll(ends, 2, 1))
    for f, (ref, out_ref) in enumerate(((s_ref, rs_ref), (a_ref, ra_ref))):
        sign = 1.0 if f == 0 else -1.0
        blk = [[block(ref, z, y) for z in range(2)] for y in range(2)]
        step_y = wide([sign * (blk[1][z] - blk[0][z]) for z in range(2)])
        for y in range(2):
            bs, hs = [], []
            for z in range(2):
                j = f * 4 + 2 * z + y
                b = blk[y][z]
                end = pltpu.roll(ends, 126 - 2 * j, 1)
                xm = jnp.where(lanes == 0, jnp.where(px == 1, end, 0.0), pltpu.roll(b, 1, 1))
                xp = jnp.where(lanes == 127, jnp.where(px == 0, end, 0.0), pltpu.roll(b, 127, 1))
                bs.append(sign * (b - xm))
                hs.append(sign * (xp - b))
            behind, ahead = wide(bs), wide(hs)
            dz = blk[y][0] - blk[y][1]
            rights = [behind if f == 0 else ahead, ahead if f == 0 else behind, wide([dz, -dz]), step_y]
            use = 4 if (y == 0) == (f == 0) else 3
            total = damp[y] * wide(blk[y])
            if f == 1:
                total = total - source[y]
            for i, r in enumerate(rights):
                k = use if i == 3 else i
                total = total + dot3(left_ref[5 * f + k, :, 0:256], split(r[0:256]), m)
                rrem_ref[32 * k : 32 * k + m - 256, :] = r[256:m]
            idle = 7 - use
            rrem_ref[32 * idle : 32 * idle + 32, :] = jnp.zeros((32, 256), F32)
            out_ref[y] = total + dot3(lrem_ref[f], split(rrem_ref[...]), m)
            g = gain if f == 0 else adgain
            out_ref[y, 0:low, :] = out_ref[y, 0:low, :] - g[:, y * 256 : (y + 1) * 256]


def first_kernel(
    par_ref, own_ref, recv_ref, n_ref, w_ref, xo_ref, xf_ref, rs_ref, ra_ref, left_ref, binv_ref, out_ref, pre_ref,
):
    m, half = rs_ref.shape[1], own_ref.shape[0] // 2
    high = up16(m)
    py, px = par_ref[0] & 1, (par_ref[0] >> 1) & 1
    row = 1 - py
    outer = par_ref[0] >> 2
    lanes = lax.broadcasted_iota(jnp.int32, (m, 128), 1)
    came = jnp.where(outer == 1, pltpu.roll(xf_ref[...], 112, 1), xo_ref[...])
    hi, lo = split(jnp.where(lanes < 16, unfold(came, m), 0.0))
    cols = (hi.astype(F32) + pltpu.roll(lo.astype(F32), 16, 1)).astype(BF16)
    edge = lanes == jnp.where(px == 0, 0, 127)
    near = n_ref.shape[0] - half
    own_o = [n_ref[0:m, :], jnp.concatenate([n_ref[half:, :], w_ref[0 : m - near, :]], axis=0)]
    for f in range(2):
        both = dot(left_ref[5 * f + (px if f == 0 else 1 - px)], cols)
        fix = both[0:m] + (pltpu.roll(both[0:m], 112, 1) + both[high : high + m])
        fix = jnp.where(px == 0, pltpu.roll(fix, 2, 1), fix) * jnp.where((px == 0) == (f == 0), -1.0, 1.0).astype(F32)
        ref = rs_ref if f == 0 else ra_ref
        fixes = [[pltpu.roll(fix, 126 - 2 * (f * 4 + 2 * z + y), 1) for y in range(2)] for z in range(2)]

        def fixed(at):
            return jnp.concatenate(
                [
                    ref[at, :, z * 128 : (z + 1) * 128]
                    + jnp.where(edge, jnp.where(at == 0, fixes[z][0], fixes[z][1]), 0.0)
                    for z in range(2)
                ],
                axis=1,
            )

        own = own_ref[f * half : f * half + m, :]
        gap = recv_ref[f * half : f * half + m, :] - own
        gap = gap * jnp.where((row == 1) == (f == 0), 1.0, -1.0).astype(F32)
        meet = 3 + row if f == 0 else 4 - row
        total = fixed(row) + dot3(left_ref[5 * f + meet], split(gap), m)
        out_ref[f] = own - 0.5 * dot3(binv_ref[f], split(total), m)
        pre_ref[f] = own_o[f] - 0.5 * dot3(binv_ref[f], split(fixed(py)), m)


def last_kernel(
    par_ref, n_ref, w_ref, recv_n_ref, recv_w_ref, recv_z_ref, pre_ref, comp_ref, done_ref, s_hbm, a_hbm,
    s_ref, a_ref, sems,
):
    m, direct = pre_ref.shape[1], n_ref.shape[0]
    half = (m + 7) // 8 * 8
    row, outer = par_ref[0] & 1, par_ref[0] >> 2
    near = direct - half
    copies = [pltpu.make_async_copy(s_ref, s_hbm, sems.at[0]), pltpu.make_async_copy(a_ref, a_hbm, sems.at[1])]
    for f, ref in enumerate((s_ref, a_ref)):
        if f == 0:
            gap = recv_n_ref[0:m, :] - n_ref[0:m, :]
        else:
            relayed = jnp.where(outer == 1, recv_z_ref[...], recv_w_ref[...]) - w_ref[...]
            gap = jnp.concatenate([recv_n_ref[half:, :] - n_ref[half:, :], relayed[0 : m - near]], axis=0)
        new = pre_ref[f] + dot3(comp_ref[f], split(gap), m)
        for z in range(2):
            here = new[:, z * 128 : (z + 1) * 128]
            there = done_ref[f, :, z * 128 : (z + 1) * 128]
            ref[pl.ds(2 * z, m, stride=4), :] = jnp.where(row == 0, here, there)
            ref[pl.ds(2 * z + 1, m, stride=4), :] = jnp.where(row == 0, there, here)
        copies[f].start()
    for c in copies:
        c.wait()


def whole(shape):
    return pl.BlockSpec(shape, lambda *_: (0,) * len(shape))


IN_HBM = pl.BlockSpec(memory_space=pltpu.HBM)


def call(kernel, scalars, args, outs, scratch=(), hbm=(), us=1.0, outs_hbm=False):
    in_specs = [IN_HBM if i in hbm else whole(x.shape) for i, x in enumerate(args)]
    args = [pltpu.with_memory_space_constraint(x, pltpu.HBM) if i in hbm else x for i, x in enumerate(args)]
    return pl.pallas_call(
        kernel,
        out_shape=outs,
        grid_spec=pltpu.PrefetchScalarGridSpec(
            num_scalar_prefetch=1,
            grid=(1,),
            in_specs=in_specs,
            out_specs=jax.tree.map(lambda o: IN_HBM if outs_hbm else whole(o.shape), outs),
            scratch_shapes=list(scratch),
        ),
        compiler_params=pltpu.CompilerParams(vmem_limit_bytes=36 * 1024 * 1024),
        cost_estimate=pl.CostEstimate(flops=int(us * 5e8), bytes_accessed=int(us * 1e6), transcendentals=0),
    )(scalars, *args)


def on_device(
    state, adjoint, upwind_pos, upwind_neg, collision, relax, wall_table, drag_weights, block_inverse,
    cell_codes, wall_mask,
):
    m, low = state.shape[0], collision.shape[0]
    half = (m + 7) // 8 * 8
    high, step = up16(m), (low + 7) // 8 * 8
    gy, gx = lax.axis_index("gy"), lax.axis_index("gx")
    ny, nx = lax.axis_size("gy"), lax.axis_size("gx")
    px = gx & 1
    spot = gy & 3
    outer = 1 - ((spot ^ (spot >> 1)) & 1)
    par = ((gy & 1) + 2 * px + 4 * outer).astype(jnp.int32).reshape(1)
    s = state.reshape(m * 4, 128)
    a = adjoint.reshape(m * 4, 128)
    sds = jax.ShapeDtypeStruct
    rowbuf = sds((2, m, 256), F32)
    colbuf = sds(((m + 31) // 32 * 8, 128), F32)
    relayed = 2 * half - DIRECT
    own_e, own_n, own_w, ends = call(
        pack_kernel, par, (s, a),
        (sds((2 * half, 256), F32), sds((DIRECT, 256), F32), sds((relayed, 256), F32), colbuf),
        (pltpu.VMEM(s.shape, F32), pltpu.VMEM(s.shape, F32), pltpu.SemaphoreType.DMA((2,))),
        hbm=(0, 1),
    )
    even = lambda n: both_ways([(i, i + 1) for i in range(0, n - 1, 2)])
    odd = lambda n: both_ways([(i, i + 1) for i in range(1, n - 1, 2)])
    quads = range(0, ny, 4)
    around = both_ways([(q, q + 3) for q in quads] + [(q + 1, q + 2) for q in quads])
    onward = [(q, q + 4) for q in quads if q + 4 < ny] + [(q + 7, q + 3) for q in quads if q + 4 < ny]
    recv_n = lax.ppermute(own_n, "gy", odd(ny))
    recv_w = lax.ppermute(own_w, "gy", around)
    recv_e = lax.ppermute(own_e, "gy", even(ny))
    recv_xe = lax.ppermute(ends, "gx", even(nx))
    ends_p = lax.ppermute(ends, "gy", even(ny))
    ends_m = call(merge_kernel, par, (ends, ends_p), colbuf)
    inner = [g for g in range(ny) if g % 4 in (1, 2)]
    recv_xo = lax.ppermute(ends_m, ("gx", "gy"), [(i * ny + g, j * ny + g) for i, j in odd(nx) for g in inner])
    recv_xf = lax.ppermute(recv_xo, "gy", even(ny))
    recv_z = lax.ppermute(recv_w, "gy", onward)
    args = (s, a, upwind_pos, upwind_neg, block_inverse, collision)
    weights = lambda n, k: sds((n, 2 * high, k), BF16)
    s_in, a_in, left, lrem, binv, comp, lcol = call(
        prep_kernel, par, args,
        (
            sds(s.shape, F32), sds(a.shape, F32), weights(10, m), weights(2, 160), weights(2, m), weights(2, m),
            sds((low * step, 128), BF16),
        ),
        (
            pltpu.VMEM((m, m), F32), pltpu.VMEM((2, 2 * high, 160), F32), pltpu.VMEM((low * step, 128), F32), pltpu.SemaphoreType.DMA((3,)),
        ),
        hbm=(0, 1, 4), us=3.0,
    )
    args = (
        s_in, a_in, left, lrem, lcol, relax, wall_table, drag_weights, cell_codes.reshape(4, 128),
        wall_mask.reshape(4, 128), recv_xe,
    )
    res_s, res_a = call(
        interior_kernel, par, args, (rowbuf, rowbuf),
        (
            pltpu.VMEM(wall_table.shape, F32), pltpu.VMEM((4, 128), jnp.int32), pltpu.VMEM((4, 128), jnp.int32),
            pltpu.VMEM((16, m), F32), pltpu.VMEM((low, 512), F32), pltpu.VMEM((160, 256), F32),
            pltpu.VMEM((low * step, 512), F32), pltpu.SemaphoreType.DMA((3,)),
        ),
        hbm=(6, 8, 9), us=4.0,
    )
    done, pre = call(
        first_kernel, par,
        (own_e, recv_e, own_n, own_w, recv_xo, recv_xf, res_s, res_a, left, binv), (rowbuf, rowbuf),
    )
    out = sds(s.shape, F32)
    s_next, a_next = call(
        last_kernel, par, (own_n, own_w, recv_n, recv_w, recv_z, pre, comp, done), (out, out),
        (pltpu.VMEM(s.shape, F32), pltpu.VMEM(s.shape, F32), pltpu.SemaphoreType.DMA((2,))), outs_hbm=True,
    )
    return s_next.reshape(state.shape), a_next.reshape(adjoint.shape)


def solution(mesh):
    field, cells = P(None, None, "gy", "gx"), P(None, "gy", "gx")
    in_specs = (field, field, P(), P(), P(), P(), P(), P(), P(), cells, cells)
    return jax.shard_map(
        on_device, mesh=mesh, in_specs=in_specs, out_specs=(field, field), check_vma=False
    )
```

time: 49.7 us -> 44 us (0.89)
  the two profiles are of different devices: /device:TPU:70 before, /device:TPU:81 now
where the time goes in v4:
time: 44 us; the launch traced here: 43.8 us
  starting transfers between devices  19.3 us (44%)
  Pallas kernels  13.7 us (31%)
  waiting for transfers between devices  9.88 us (22%)
  between operations  0.82 us (2%)
    pallas_call x6, Pallas kernels, call(): pl.pallas_call(kernel, out_shape=outs, grid_spec=pltpu.PrefetchScalarGrid...  13.7 us
    ppermute x1, waiting for transfers between devices, on_device(): ends_p = lax.ppermute(ends, 'gy', even(ny))  7.62 us
    ppermute x1, starting transfers between devices, on_device(): recv_z = lax.ppermute(recv_w, 'gy', onward)  6.1 us
    ppermute x1, starting transfers between devices, on_device(): recv_xf = lax.ppermute(recv_xo, 'gy', even(ny))  4.96 us
    ppermute x1, starting transfers between devices, on_device(): recv_w = lax.ppermute(own_w, 'gy', around)  2.48 us
    ppermute x1, waiting for transfers between devices, on_device(): recv_z = lax.ppermute(recv_w, 'gy', onward)  2.24 us
    ppermute x1, starting transfers between devices, on_device(): recv_n = lax.ppermute(own_n, 'gy', odd(ny))  1.91 us
    ppermute x1, starting transfers between devices, on_device(): recv_xe = lax.ppermute(ends, 'gx', even(nx))  1.52 us
  transfers between devices with their start and end apart: 8, of which 2 were waited for; matrix products, arithmetic and copies ran while one was open for 0% of the time, Pallas kernels for 24%

profile of v4, /device:TPU:81, one launch (start us, length us, event | category | flops | bytes accessed | tf_op | source)
XLA Modules:
  0.0 43.8 jit_solution(11365591950566849759)
XLA Ops:
  0.6 0.0 copy-start.1
  0.7 0.0 copy-start.2
  0.7 1.7 %shard_map.122 = (f32[576,256]{1,0:T(8,128)S(1)}, f32[376,256]{1,0:T(8,128)S(1)}, f32[200,256]{1,0:T(8,128)S(1)}, f32[72,128]{1,0:T(8,128)S(1)}) custom-call(s32[1]{0:T(128)} %bitcast.par_ref, f32[1144,128]{1,0:T(8,128)} %bitcast.7, f32[1144,128]{1,0:T(8,128)} %bitcast.9), custom_call_target="tpu_custom_call" | custom-call | flops 500000000 | bytes 1000000 | tf_op jit(solution)/shard_map/pallas_call | solution.py:302
  2.4 0.0 copy-start
  2.4 1.3 %collective-permute-start.3 = (f32[576,256]{1,0:T(8,128)S(1)}, f32[576,256]{1,0:T(8,128)S(1)}, u32[]{:S(2)}, u32[]{:S(2)}) collective-permute-start(f32[576,256]{1,0:T(8,128)S(1)} %get-tuple-element.21.own_ref), channel_id=1, source_target_pairs={{0,1},{2,3},{4,5},{6,7},{8,9},{10,11},{12,13},{14,15},{1,0},{3,2},... | collective-permute-start | bytes 1769480 | tf_op jit(solution)/shard_map/ppermute | solution.py:349
  3.7 0.3 collective-permute-start.4
  4.0 2.5 %collective-permute-start.1 = (f32[200,256]{1,0:T(8,128)S(1)}, f32[200,256]{1,0:T(8,128)S(1)}, u32[]{:S(2)}, u32[]{:S(2)}) collective-permute-start(f32[200,256]{1,0:T(8,128)S(1)} %get-tuple-element.20.w_ref), channel_id=1, source_target_pairs={{0,3},{4,7},{8,11},{12,15},{1,2},{5,6},{9,10},{13,14},{3,0},{7,4},... | collective-permute-start | bytes 614408 | tf_op jit(solution)/shard_map/ppermute | solution.py:348
  6.4 1.5 %collective-permute-start.7 = (f32[72,128]{1,0:T(8,128)S(1)}, f32[72,128]{1,0:T(8,128)S(1)}, u32[]{:S(2)}, u32[]{:S(2)}) collective-permute-start(f32[72,128]{1,0:T(8,128)S(1)} %get-tuple-element.22.own_ref), channel_id=1, source_target_pairs={{0,16},{32,48},{64,80},{96,112},{128,144},{160,176},{192,208},{224... | collective-permute-start | bytes 110600 | tf_op jit(solution)/shard_map/ppermute | solution.py:350
  8.0 1.9 %collective-permute-start = (f32[376,256]{1,0:T(8,128)S(1)}, f32[376,256]{1,0:T(8,128)S(1)}, u32[]{:S(2)}, u32[]{:S(2)}) collective-permute-start(f32[376,256]{1,0:T(8,128)S(1)} %get-tuple-element.19.n_ref), channel_id=1, source_target_pairs={{1,2},{3,4},{5,6},{7,8},{9,10},{11,12},{13,14},{2,1},{4,3},{6,5},{... | collective-permute-start | bytes 1155080 | tf_op jit(solution)/shard_map/ppermute | solution.py:347
  9.9 7.6 %collective-permute-done.4.other_ref = f32[72,128]{1,0:T(8,128)S(1)} collective-permute-done((f32[72,128]{1,0:T(8,128)S(1)}, f32[72,128]{1,0:T(8,128)S(1)}, u32[]{:S(2)}, u32[]{:S(2)}) %collective-permute-start.4) | collective-permute-done | bytes 36896 | tf_op jit(solution)/shard_map/ppermute | solution.py:351
  17.5 0.1 shard_map.123
  17.6 0.0 copy-start.3
  17.6 0.0 copy-start.4
  17.6 0.8 %collective-permute-start.5 = (f32[72,128]{1,0:T(8,128)S(1)}, f32[72,128]{1,0:T(8,128)S(1)}, u32[]{:S(2)}, u32[]{:S(2)}) collective-permute-start(f32[72,128]{1,0:T(8,128)S(1)} %shard_map.123), channel_id=1, source_target_pairs={{17,33},{18,34},{21,37},{22,38},{25,41},{26,42},{29,45},{30,46},{4... | collective-permute-start | bytes 110600 | tf_op jit(solution)/shard_map/ppermute | solution.py:354
  18.4 0.0 copy-done.1
  18.4 0.0 copy-done.2
  18.4 0.0 copy-done
  18.4 3.4 %shard_map.124 = (f32[1144,128]{1,0:T(8,128)S(1)}, f32[1144,128]{1,0:T(8,128)S(1)}, bf16[10,576,286]{2,1,0:T(8,128)(2,1)S(1)}, bf16[2,576,160]{2,1,0:T(8,128)(2,...) custom-call(s32[1]{0:T(128)} %bitcast.par_ref, ...), custom_call_target="tpu_custom_call" | custom-call | flops 1500000000 | bytes 3000000 | tf_op jit(solution)/shard_map/pallas_call | solution.py:302
  21.8 0.0 collective-permute-done.5.xo_ref
  21.8 5.0 %collective-permute-start.6 = (f32[72,128]{1,0:T(8,128)S(1)}, f32[72,128]{1,0:T(8,128)S(1)}, u32[]{:S(2)}, u32[]{:S(2)}) collective-permute-start(f32[72,128]{1,0:T(8,128)S(1)} %collective-permute-done.5.xo_ref), channel_id=1, source_target_pairs={{0,1},{2,3},{4,5},{6,7},{8,9},{10,11},{12,13},{14,15},{1,0},{3,2},... | collective-permute-start | bytes 110600 | tf_op jit(solution)/shard_map/ppermute | solution.py:355
  26.8 0.0 collective-permute-done.1.recv_w_ref
  26.8 6.1 %collective-permute-start.2 = (f32[200,256]{1,0:T(8,128)S(1)}, f32[200,256]{1,0:T(8,128)S(1)}, u32[]{:S(2)}, u32[]{:S(2)}) collective-permute-start(f32[200,256]{1,0:T(8,128)S(1)} %collective-permute-done.1.recv_w_ref), channel_id=1, source_target_pairs={{0,4},{4,8},{8,12},{7,3},{11,7},{15,11},{16,20},{20,24},{24,28},{2... | collective-permute-start | bytes 614408 | tf_op jit(solution)/shard_map/ppermute | solution.py:356
  32.9 0.0 collective-permute-done.7.xe_ref
  32.9 0.0 copy-done.3
  32.9 0.0 copy-done.4
  33.0 3.9 %shard_map.125 = (f32[2,286,256]{2,1,0:T(8,128)S(1)}, f32[2,286,256]{2,1,0:T(8,128)S(1)}) custom-call(s32[1]{0:T(128)} %bitcast.par_ref, f32[1144,128]{1,0:T(8,128)S(1)} %get-tuple-element.23.s_ref, f32[1144,128]{1,0:T(8,128)S(1)} %get-tuple-element.24.a_ref, bf16[10,576,286]{2,1,0:T(8,128)(2,1)S(1)} %get-tuple-element.25.left_ref, ...), custom_call_target="tpu_custom_call" | custom-call | flops 2000000000 | bytes 4000000 | tf_op jit(solution)/shard_map/pallas_call | solution.py:302
  36.9 0.0 collective-permute-done.6.xf_ref
  36.9 0.0 collective-permute-done.3.recv_ref
  36.9 2.9 %shard_map.126 = (f32[2,286,256]{2,1,0:T(8,128)S(1)}, f32[2,286,256]{2,1,0:T(8,128)S(1)}) custom-call(s32[1]{0:T(128)} %bitcast.par_ref, f32[576,256]{1,0:T(8,128)S(1)} %get-tuple-element.21.own_ref, f32[576,256]{1,0:T(8,128)S(1)} %collective-permute-done.3.recv_ref, f32[376,256]{1,0:T(8,128)S(1)} %get-tuple-element.19.n_ref, ...), custom_call_target="tpu_custom_call" | custom-call | flops 500000000 | bytes 1000000 | tf_op jit(solution)/shard_map/pallas_call | solution.py:302
  39.8 0.0 collective-permute-done.recv_n_ref
  39.8 2.2 %collective-permute-done.2.recv_z_ref = f32[200,256]{1,0:T(8,128)S(1)} collective-permute-done((f32[200,256]{1,0:T(8,128)S(1)}, f32[200,256]{1,0:T(8,128)S(1)}, u32[]{:S(2)}, u32[]{:S(2)}) %collective-permute-start.2) | collective-permute-done | bytes 204832 | tf_op jit(solution)/shard_map/ppermute | solution.py:356
  42.1 1.7 %shard_map.127 = (f32[1144,128]{1,0:T(8,128)}, f32[1144,128]{1,0:T(8,128)}) custom-call(s32[1]{0:T(128)} %bitcast.par_ref, f32[376,256]{1,0:T(8,128)S(1)} %get-tuple-element.19.n_ref, f32[200,256]{1,0:T(8,128)S(1)} %get-tuple-element.20.w_ref, f32[376,256]{1,0:T(8,128)S(1)} %collective-permute-done.recv_n_ref, ...), custom_call_target="tpu_custom_call" | custom-call | flops 500000000 | bytes 1000000 | tf_op jit(solution)/shard_map/pallas_call | solution.py:302
Async XLA Ops:
  0.6 17.8 %copy-start.1 = (f32[3,286,286]{2,1,0:T(8,128)S(1)}, f32[3,286,286]{2,1,0:T(8,128)}, u32[]{:S(2)}) copy-start(f32[3,286,286]{2,1,0:T(8,128)} %un_ref.1) | copy-start | bytes 2944660
  0.7 17.8 %copy-start.2 = (f32[35,35,35]{2,1,0:T(8,128)S(1)}, f32[35,35,35]{2,1,0:T(8,128)}, u32[]{:S(2)}) copy-start(f32[35,35,35]{2,1,0:T(8,128)} %col_ref.1) | copy-start | bytes 514504
  2.4 16.0 %copy-start = (f32[3,286,286]{2,1,0:T(8,128)S(1)}, f32[3,286,286]{2,1,0:T(8,128)}, u32[]{:S(2)}) copy-start(f32[3,286,286]{2,1,0:T(8,128)} %up_ref.1) | copy-start | bytes 2944660
  2.4 34.5 %collective-permute-start.3 = (f32[576,256]{1,0:T(8,128)S(1)}, f32[576,256]{1,0:T(8,128)S(1)}, u32[]{:S(2)}, u32[]{:S(2)}) collective-permute-start(f32[576,256]{1,0:T(8,128)S(1)} %get-tuple-element.21.own_ref), channel_id=1, source_target_pairs={{0,1},{2,3},{4,5},{6,7},{8,9},{10,11},{12,13},{14,15},{1,0},{3,2},... | collective-permute-start | bytes 1769480 | tf_op jit(solution)/shard_map/ppermute | solution.py:349
  3.7 13.8 %collective-permute-start.4 = (f32[72,128]{1,0:T(8,128)S(1)}, f32[72,128]{1,0:T(8,128)S(1)}, u32[]{:S(2)}, u32[]{:S(2)}) collective-permute-start(f32[72,128]{1,0:T(8,128)S(1)} %get-tuple-element.22.own_ref), channel_id=1, source_target_pairs={{0,1},{2,3},{4,5},{6,7},{8,9},{10,11},{12,13},{14,15},{1,0},{3,2},... | collective-permute-start | bytes 110600 | tf_op jit(solution)/shard_map/ppermute | solution.py:351
  4.0 22.8 %collective-permute-start.1 = (f32[200,256]{1,0:T(8,128)S(1)}, f32[200,256]{1,0:T(8,128)S(1)}, u32[]{:S(2)}, u32[]{:S(2)}) collective-permute-start(f32[200,256]{1,0:T(8,128)S(1)} %get-tuple-element.20.w_ref), channel_id=1, source_target_pairs={{0,3},{4,7},{8,11},{12,15},{1,2},{5,6},{9,10},{13,14},{3,0},{7,4},... | collective-permute-start | bytes 614408 | tf_op jit(solution)/shard_map/ppermute | solution.py:348
  6.4 26.5 %collective-permute-start.7 = (f32[72,128]{1,0:T(8,128)S(1)}, f32[72,128]{1,0:T(8,128)S(1)}, u32[]{:S(2)}, u32[]{:S(2)}) collective-permute-start(f32[72,128]{1,0:T(8,128)S(1)} %get-tuple-element.22.own_ref), channel_id=1, source_target_pairs={{0,16},{32,48},{64,80},{96,112},{128,144},{160,176},{192,208},{224... | collective-permute-start | bytes 110600 | tf_op jit(solution)/shard_map/ppermute | solution.py:350
  8.0 31.9 %collective-permute-start = (f32[376,256]{1,0:T(8,128)S(1)}, f32[376,256]{1,0:T(8,128)S(1)}, u32[]{:S(2)}, u32[]{:S(2)}) collective-permute-start(f32[376,256]{1,0:T(8,128)S(1)} %get-tuple-element.19.n_ref), channel_id=1, source_target_pairs={{1,2},{3,4},{5,6},{7,8},{9,10},{11,12},{13,14},{2,1},{4,3},{6,5},{... | collective-permute-start | bytes 1155080 | tf_op jit(solution)/shard_map/ppermute | solution.py:347
  17.6 15.4 %copy-start.3 = (f32[286]{0:T(512)S(1)}, f32[286]{0:T(512)}, u32[]{:S(2)}) copy-start(f32[286]{0:T(512)} %relax_ref.1) | copy-start | bytes 3436
  17.6 15.4 %copy-start.4 = (f32[286]{0:T(512)S(1)}, f32[286]{0:T(512)}, u32[]{:S(2)}) copy-start(f32[286]{0:T(512)} %dw_ref.1) | copy-start | bytes 3436
  17.6 4.2 %collective-permute-start.5 = (f32[72,128]{1,0:T(8,128)S(1)}, f32[72,128]{1,0:T(8,128)S(1)}, u32[]{:S(2)}, u32[]{:S(2)}) collective-permute-start(f32[72,128]{1,0:T(8,128)S(1)} %shard_map.123), channel_id=1, source_target_pairs={{17,33},{18,34},{21,37},{22,38},{25,41},{26,42},{29,45},{30,46},{4... | collective-permute-start | bytes 110600 | tf_op jit(solution)/shard_map/ppermute | solution.py:354
  21.8 15.0 %collective-permute-start.6 = (f32[72,128]{1,0:T(8,128)S(1)}, f32[72,128]{1,0:T(8,128)S(1)}, u32[]{:S(2)}, u32[]{:S(2)}) collective-permute-start(f32[72,128]{1,0:T(8,128)S(1)} %collective-permute-done.5.xo_ref), channel_id=1, source_target_pairs={{0,1},{2,3},{4,5},{6,7},{8,9},{10,11},{12,13},{14,15},{1,0},{3,2},... | collective-permute-start | bytes 110600 | tf_op jit(solution)/shard_map/ppermute | solution.py:355
  26.8 15.2 %collective-permute-start.2 = (f32[200,256]{1,0:T(8,128)S(1)}, f32[200,256]{1,0:T(8,128)S(1)}, u32[]{:S(2)}, u32[]{:S(2)}) collective-permute-start(f32[200,256]{1,0:T(8,128)S(1)} %collective-permute-done.1.recv_w_ref), channel_id=1, source_target_pairs={{0,4},{4,8},{8,12},{7,3},{11,7},{15,11},{16,20},{20,24},{24,28},{2... | collective-permute-start | bytes 614408 | tf_op jit(solution)/shard_map/ppermute | solution.py:356

commit v5 on v4

--- a/solution.py
+++ b/solution.py
@@ -8,7 +8,7 @@
 
 F32 = jnp.float32
 BF16 = jnp.bfloat16
-DIRECT = 376
+DIRECT = 368
 
 
 def both_ways(pairs):
@@ -33,6 +33,13 @@
     high = up16(m)
     both = dot(left, b[0])
     return both[0:m, :] + (both[high : high + m, :] + dot(left[0:m, :], b[1]))
+
+
+def dot3_tail(left, rem, b, m):
+    tail = jnp.concatenate([b[256:m], jnp.zeros((32 - (m - 256), b.shape[1]), F32)], axis=0)
+    hi, lo = split(tail)
+    right = jnp.concatenate([hi, hi, lo, jnp.zeros_like(hi)], axis=0)
+    return dot3(left[:, 0:256], split(b[0:256]), m) + dot(rem, right)
 
 
 def fetch(pairs, sems):
@@ -86,8 +93,8 @@
 
 def prep_kernel(
     par_ref, s_hbm, a_hbm, up_ref, un_ref, b_hbm, col_ref,
-    s_ref, a_ref, left_ref, lrem_ref, binv_ref, comp_ref, lcol_ref,
-    b_ref, rem_ref, cmat_ref, sems,
+    s_ref, a_ref, left_ref, lrem_ref, binv_ref, comp_ref, lcol_ref, tail_ref,
+    b_ref, pad_ref, rem_ref, cmat_ref, sems,
 ):
     m = b_ref.shape[0]
     high = up16(m)
@@ -112,15 +119,28 @@
             rem_ref[f, high : high + m, 32 * i : 32 * i + m - 256] = lo[:, 256:].astype(F32)
         lrem_ref[f] = rem_ref[f].astype(BF16)
         meets.append(jnp.where((row == 0) == (f == 0), mats[3], mats[4]))
+    pad_ref[...] = jnp.zeros_like(pad_ref)
+
+    def keep_tail(at, hi, lo):
+        pad_ref[:, 0 : m - 256] = hi[:, 256:].astype(F32)
+        pad_ref[:, 32 : 32 + m - 256] = lo[:, 256:].astype(F32)
+        pad_ref[:, 64 : 64 + m - 256] = hi[:, 256:].astype(F32)
+        tail_ref[at] = pad_ref[...].astype(BF16)
+
+    for f in range(2):
+        for i in range(2):
+            keep_tail(2 * f + i, left_ref[5 * f + 3 + i, 0:m, :], left_ref[5 * f + 3 + i, high : high + m, :])
     copies[0].wait()
     for f in range(2):
         hi, lo = split(b_ref[...] if f == 0 else b_ref[...].T)
         binv_ref[f, 0:m, :] = hi
         binv_ref[f, high : high + m, :] = lo
+        keep_tail(4 + f, hi, lo)
         scale = jnp.where((row == 1) == (f == 0), -0.5, 0.5).astype(F32)
         hi, lo = split(scale * dot3(binv_ref[f], split(meets[f]), m))
         comp_ref[f, 0:m, :] = hi
         comp_ref[f, high : high + m, :] = lo
+        keep_tail(6 + f, hi, lo)
     for k in range(low):
         c = col_ref[k]
         c = c + c.T
@@ -223,7 +243,7 @@
 
 
 def first_kernel(
-    par_ref, own_ref, recv_ref, n_ref, w_ref, xo_ref, xf_ref, rs_ref, ra_ref, left_ref, binv_ref, out_ref, pre_ref,
+    par_ref, own_ref, recv_ref, n_ref, w_ref, xo_ref, xf_ref, rs_ref, ra_ref, left_ref, binv_ref, tail_ref, out_ref, pre_ref,
 ):
     m, half = rs_ref.shape[1], own_ref.shape[0] // 2
     high = up16(m)
@@ -258,13 +278,13 @@
         gap = recv_ref[f * half : f * half + m, :] - own
         gap = gap * jnp.where((row == 1) == (f == 0), 1.0, -1.0).astype(F32)
         meet = 3 + row if f == 0 else 4 - row
-        total = fixed(row) + dot3(left_ref[5 * f + meet], split(gap), m)
-        out_ref[f] = own - 0.5 * dot3(binv_ref[f], split(total), m)
-        pre_ref[f] = own_o[f] - 0.5 * dot3(binv_ref[f], split(fixed(py)), m)
+        total = fixed(row) + dot3_tail(left_ref.at[5 * f + meet], tail_ref[2 * f + meet - 3], gap, m)
+        out_ref[f] = own - 0.5 * dot3_tail(binv_ref.at[f], tail_ref[4 + f], total, m)
+        pre_ref[f] = own_o[f] - 0.5 * dot3_tail(binv_ref.at[f], tail_ref[4 + f], fixed(py), m)
 
 
 def last_kernel(
-    par_ref, n_ref, w_ref, recv_n_ref, recv_w_ref, recv_z_ref, pre_ref, comp_ref, done_ref, s_hbm, a_hbm,
+    par_ref, n_ref, w_ref, recv_n_ref, recv_w_ref, recv_z_ref, pre_ref, comp_ref, tail_ref, done_ref, s_hbm, a_hbm,
     s_ref, a_ref, sems,
 ):
     m, direct = pre_ref.shape[1], n_ref.shape[0]
@@ -278,7 +298,7 @@
         else:
             relayed = jnp.where(outer == 1, recv_z_ref[...], recv_w_ref[...]) - w_ref[...]
             gap = jnp.concatenate([recv_n_ref[half:, :] - n_ref[half:, :], relayed[0 : m - near]], axis=0)
-        new = pre_ref[f] + dot3(comp_ref[f], split(gap), m)
+        new = pre_ref[f] + dot3_tail(comp_ref.at[f], tail_ref[6 + f], gap, m)
         for z in range(2):
             here = new[:, z * 128 : (z + 1) * 128]
             there = done_ref[f, :, z * 128 : (z + 1) * 128]
@@ -356,14 +376,14 @@
     recv_z = lax.ppermute(recv_w, "gy", onward)
     args = (s, a, upwind_pos, upwind_neg, block_inverse, collision)
     weights = lambda n, k: sds((n, 2 * high, k), BF16)
-    s_in, a_in, left, lrem, binv, comp, lcol = call(
+    s_in, a_in, left, lrem, binv, comp, lcol, tails = call(
         prep_kernel, par, args,
         (
             sds(s.shape, F32), sds(a.shape, F32), weights(10, m), weights(2, 160), weights(2, m), weights(2, m),
-            sds((low * step, 128), BF16),
+            sds((low * step, 128), BF16), sds((8, m, 128), BF16),
         ),
         (
-            pltpu.VMEM((m, m), F32), pltpu.VMEM((2, 2 * high, 160), F32), pltpu.VMEM((low * step, 128), F32), pltpu.SemaphoreType.DMA((3,)),
+            pltpu.VMEM((m, m), F32), pltpu.VMEM((m, 128), F32), pltpu.VMEM((2, 2 * high, 160), F32), pltpu.VMEM((low * step, 128), F32), pltpu.SemaphoreType.DMA((3,)),
         ),
         hbm=(0, 1, 4), us=3.0,
     )
@@ -382,11 +402,11 @@
     )
     done, pre = call(
         first_kernel, par,
-        (own_e, recv_e, own_n, own_w, recv_xo, recv_xf, res_s, res_a, left, binv), (rowbuf, rowbuf),
+        (own_e, recv_e, own_n, own_w, recv_xo, recv_xf, res_s, res_a, left, binv, tails), (rowbuf, rowbuf),
     )
     out = sds(s.shape, F32)
     s_next, a_next = call(
-        last_kernel, par, (own_n, own_w, recv_n, recv_w, recv_z, pre, comp, done), (out, out),
+        last_kernel, par, (own_n, own_w, recv_n, recv_w, recv_z, pre, comp, tails, done), (out, out),
         (pltpu.VMEM(s.shape, F32), pltpu.VMEM(s.shape, F32), pltpu.SemaphoreType.DMA((2,))), outs_hbm=True,
     )
     return s_next.reshape(state.shape), a_next.reshape(adjoint.shape)

time: 44 us -> 44.2 us (level)
  waiting for transfers between devices: 9.88 us -> 10.9 us
  Pallas kernels: 13.7 us -> 12.9 us
    ppermute x1, waiting for transfers between devices: 2.24 us -> 3.3 us  [on_device(): recv_z = lax.ppermute(recv_w, 'gy', onward)]
    pallas_call x6, Pallas kernels: 13.7 us -> 12.9 us  [call(): pl.pallas_call(kernel, out_shape=outs, grid_spec=pltpu.PrefetchScalarGrid...]
  transfers between devices with their start and end apart: 8 -> 8, of which waited for: 2 -> 2; matrix products, arithmetic and copies ran while one was open for 0% -> 0% of each run, Pallas kernels for 24% -> 22%
where the time goes in v5:
time: 44.2 us; the launch traced here: 44 us
  starting transfers between devices  19.3 us (44%)
  Pallas kernels  12.9 us (29%)
  waiting for transfers between devices  10.9 us (25%)
  between operations  0.82 us (2%)
    pallas_call x6, Pallas kernels, call(): pl.pallas_call(kernel, out_shape=outs, grid_spec=pltpu.PrefetchScalarGrid...  12.9 us
    ppermute x1, waiting for transfers between devices, on_device(): ends_p = lax.ppermute(ends, 'gy', even(ny))  7.62 us
    ppermute x1, starting transfers between devices, on_device(): recv_z = lax.ppermute(recv_w, 'gy', onward)  6.1 us
    ppermute x1, starting transfers between devices, on_device(): recv_xf = lax.ppermute(recv_xo, 'gy', even(ny))  4.96 us
    ppermute x1, waiting for transfers between devices, on_device(): recv_z = lax.ppermute(recv_w, 'gy', onward)  3.3 us
    ppermute x1, starting transfers between devices, on_device(): recv_w = lax.ppermute(own_w, 'gy', around)  2.48 us
    ppermute x1, starting transfers between devices, on_device(): recv_n = lax.ppermute(own_n, 'gy', odd(ny))  1.91 us
    ppermute x1, starting transfers between devices, on_device(): recv_xe = lax.ppermute(ends, 'gx', even(nx))  1.52 us
  transfers between devices with their start and end apart: 8, of which 2 were waited for; matrix products, arithmetic and copies ran while one was open for 0% of the time, Pallas kernels for 22%

profile of v5, /device:TPU:81, one launch (start us, length us, event | category | flops | bytes accessed | tf_op | source)
XLA Modules:
  0.0 44.0 jit_solution(4706065607404877248)
XLA Ops:
  0.6 0.0 copy-start.1
  0.7 0.0 copy-start.2
  0.7 1.7 %shard_map.122 = (f32[576,256]{1,0:T(8,128)S(1)}, f32[368,256]{1,0:T(8,128)S(1)}, f32[208,256]{1,0:T(8,128)S(1)}, f32[72,128]{1,0:T(8,128)S(1)}) custom-call(s32[1]{0:T(128)} %bitcast.par_ref, f32[1144,128]{1,0:T(8,128)} %bitcast.7, f32[1144,128]{1,0:T(8,128)} %bitcast.9), custom_call_target="tpu_custom_call" | custom-call | flops 500000000 | bytes 1000000 | tf_op jit(solution)/shard_map/pallas_call | solution.py:322
  2.4 0.0 copy-start
  2.4 1.3 %collective-permute-start.3 = (f32[576,256]{1,0:T(8,128)S(1)}, f32[576,256]{1,0:T(8,128)S(1)}, u32[]{:S(2)}, u32[]{:S(2)}) collective-permute-start(f32[576,256]{1,0:T(8,128)S(1)} %get-tuple-element.22.own_ref), channel_id=1, source_target_pairs={{0,1},{2,3},{4,5},{6,7},{8,9},{10,11},{12,13},{14,15},{1,0},{3,2},... | collective-permute-start | bytes 1769480 | tf_op jit(solution)/shard_map/ppermute | solution.py:369
  3.7 0.3 collective-permute-start.4
  4.0 2.5 %collective-permute-start.1 = (f32[208,256]{1,0:T(8,128)S(1)}, f32[208,256]{1,0:T(8,128)S(1)}, u32[]{:S(2)}, u32[]{:S(2)}) collective-permute-start(f32[208,256]{1,0:T(8,128)S(1)} %get-tuple-element.21.w_ref), channel_id=1, source_target_pairs={{0,3},{4,7},{8,11},{12,15},{1,2},{5,6},{9,10},{13,14},{3,0},{7,4},... | collective-permute-start | bytes 638984 | tf_op jit(solution)/shard_map/ppermute | solution.py:368
  6.4 1.5 %collective-permute-start.7 = (f32[72,128]{1,0:T(8,128)S(1)}, f32[72,128]{1,0:T(8,128)S(1)}, u32[]{:S(2)}, u32[]{:S(2)}) collective-permute-start(f32[72,128]{1,0:T(8,128)S(1)} %get-tuple-element.23.own_ref), channel_id=1, source_target_pairs={{0,16},{32,48},{64,80},{96,112},{128,144},{160,176},{192,208},{224... | collective-permute-start | bytes 110600 | tf_op jit(solution)/shard_map/ppermute | solution.py:370
  8.0 1.9 %collective-permute-start = (f32[368,256]{1,0:T(8,128)S(1)}, f32[368,256]{1,0:T(8,128)S(1)}, u32[]{:S(2)}, u32[]{:S(2)}) collective-permute-start(f32[368,256]{1,0:T(8,128)S(1)} %get-tuple-element.20.n_ref), channel_id=1, source_target_pairs={{1,2},{3,4},{5,6},{7,8},{9,10},{11,12},{13,14},{2,1},{4,3},{6,5},{... | collective-permute-start | bytes 1130504 | tf_op jit(solution)/shard_map/ppermute | solution.py:367
  9.9 7.6 %collective-permute-done.4.other_ref = f32[72,128]{1,0:T(8,128)S(1)} collective-permute-done((f32[72,128]{1,0:T(8,128)S(1)}, f32[72,128]{1,0:T(8,128)S(1)}, u32[]{:S(2)}, u32[]{:S(2)}) %collective-permute-start.4) | collective-permute-done | bytes 36896 | tf_op jit(solution)/shard_map/ppermute | solution.py:371
  17.5 0.1 shard_map.123
  17.6 0.0 copy-start.3
  17.6 0.0 copy-start.4
  17.6 0.8 %collective-permute-start.5 = (f32[72,128]{1,0:T(8,128)S(1)}, f32[72,128]{1,0:T(8,128)S(1)}, u32[]{:S(2)}, u32[]{:S(2)}) collective-permute-start(f32[72,128]{1,0:T(8,128)S(1)} %shard_map.123), channel_id=1, source_target_pairs={{17,33},{18,34},{21,37},{22,38},{25,41},{26,42},{29,45},{30,46},{4... | collective-permute-start | bytes 110600 | tf_op jit(solution)/shard_map/ppermute | solution.py:374
  18.4 0.0 copy-done.1
  18.4 0.0 copy-done.2
  18.4 0.0 copy-done
  18.4 3.5 %shard_map.124 = (f32[1144,128]{1,0:T(8,128)S(1)}, f32[1144,128]{1,0:T(8,128)S(1)}, bf16[10,576,286]{2,1,0:T(8,128)(2,1)S(1)}, bf16[2,576,160]{2,1,0:T(8,128)(2,...) custom-call(s32[1]{0:T(128)} %bitcast.par_ref, ...), custom_call_target="tpu_custom_call" | custom-call | flops 1500000000 | bytes 3000000 | tf_op jit(solution)/shard_map/pallas_call | solution.py:322
  21.9 0.0 collective-permute-done.5.xo_ref
  21.9 5.0 %collective-permute-start.6 = (f32[72,128]{1,0:T(8,128)S(1)}, f32[72,128]{1,0:T(8,128)S(1)}, u32[]{:S(2)}, u32[]{:S(2)}) collective-permute-start(f32[72,128]{1,0:T(8,128)S(1)} %collective-permute-done.5.xo_ref), channel_id=1, source_target_pairs={{0,1},{2,3},{4,5},{6,7},{8,9},{10,11},{12,13},{14,15},{1,0},{3,2},... | collective-permute-start | bytes 110600 | tf_op jit(solution)/shard_map/ppermute | solution.py:375
  26.9 0.0 collective-permute-done.1.recv_w_ref
  26.9 6.1 %collective-permute-start.2 = (f32[208,256]{1,0:T(8,128)S(1)}, f32[208,256]{1,0:T(8,128)S(1)}, u32[]{:S(2)}, u32[]{:S(2)}) collective-permute-start(f32[208,256]{1,0:T(8,128)S(1)} %collective-permute-done.1.recv_w_ref), channel_id=1, source_target_pairs={{0,4},{4,8},{8,12},{7,3},{11,7},{15,11},{16,20},{20,24},{24,28},{2... | collective-permute-start | bytes 638984 | tf_op jit(solution)/shard_map/ppermute | solution.py:376
  33.0 0.0 collective-permute-done.7.xe_ref
  33.0 0.0 copy-done.3
  33.0 0.0 copy-done.4
  33.0 3.9 %shard_map.125 = (f32[2,286,256]{2,1,0:T(8,128)S(1)}, f32[2,286,256]{2,1,0:T(8,128)S(1)}) custom-call(s32[1]{0:T(128)} %bitcast.par_ref, f32[1144,128]{1,0:T(8,128)S(1)} %get-tuple-element.24.s_ref, f32[1144,128]{1,0:T(8,128)S(1)} %get-tuple-element.25.a_ref, bf16[10,576,286]{2,1,0:T(8,128)(2,1)S(1)} %get-tuple-element.26.left_ref, ...), custom_call_target="tpu_custom_call" | custom-call | flops 2000000000 | bytes 4000000 | tf_op jit(solution)/shard_map/pallas_call | solution.py:322
  36.9 0.0 collective-permute-done.6.xf_ref
  36.9 0.0 collective-permute-done.3.recv_ref
  36.9 2.2 %shard_map.126 = (f32[2,286,256]{2,1,0:T(8,128)S(1)}, f32[2,286,256]{2,1,0:T(8,128)S(1)}) custom-call(s32[1]{0:T(128)} %bitcast.par_ref, f32[576,256]{1,0:T(8,128)S(1)} %get-tuple-element.22.own_ref, f32[576,256]{1,0:T(8,128)S(1)} %collective-permute-done.3.recv_ref, f32[368,256]{1,0:T(8,128)S(1)} %get-tuple-element.20.n_ref, ...), custom_call_target="tpu_custom_call" | custom-call | flops 500000000 | bytes 1000000 | tf_op jit(solution)/shard_map/pallas_call | solution.py:322
  39.2 0.0 collective-permute-done.recv_n_ref
  39.2 3.3 %collective-permute-done.2.recv_z_ref = f32[208,256]{1,0:T(8,128)S(1)} collective-permute-done((f32[208,256]{1,0:T(8,128)S(1)}, f32[208,256]{1,0:T(8,128)S(1)}, u32[]{:S(2)}, u32[]{:S(2)}) %collective-permute-start.2) | collective-permute-done | bytes 213024 | tf_op jit(solution)/shard_map/ppermute | solution.py:376
  42.5 1.5 %shard_map.127 = (f32[1144,128]{1,0:T(8,128)}, f32[1144,128]{1,0:T(8,128)}) custom-call(s32[1]{0:T(128)} %bitcast.par_ref, f32[368,256]{1,0:T(8,128)S(1)} %get-tuple-element.20.n_ref, f32[208,256]{1,0:T(8,128)S(1)} %get-tuple-element.21.w_ref, f32[368,256]{1,0:T(8,128)S(1)} %collective-permute-done.recv_n_ref, ...), custom_call_target="tpu_custom_call" | custom-call | flops 500000000 | bytes 1000000 | tf_op jit(solution)/shard_map/pallas_call | solution.py:322
Async XLA Ops:
  0.6 17.8 %copy-start.1 = (f32[3,286,286]{2,1,0:T(8,128)S(1)}, f32[3,286,286]{2,1,0:T(8,128)}, u32[]{:S(2)}) copy-start(f32[3,286,286]{2,1,0:T(8,128)} %un_ref.1) | copy-start | bytes 2944660
  0.7 17.8 %copy-start.2 = (f32[35,35,35]{2,1,0:T(8,128)S(1)}, f32[35,35,35]{2,1,0:T(8,128)}, u32[]{:S(2)}) copy-start(f32[35,35,35]{2,1,0:T(8,128)} %col_ref.1) | copy-start | bytes 514504
  2.4 16.0 %copy-start = (f32[3,286,286]{2,1,0:T(8,128)S(1)}, f32[3,286,286]{2,1,0:T(8,128)}, u32[]{:S(2)}) copy-start(f32[3,286,286]{2,1,0:T(8,128)} %up_ref.1) | copy-start | bytes 2944660
  2.4 34.5 %collective-permute-start.3 = (f32[576,256]{1,0:T(8,128)S(1)}, f32[576,256]{1,0:T(8,128)S(1)}, u32[]{:S(2)}, u32[]{:S(2)}) collective-permute-start(f32[576,256]{1,0:T(8,128)S(1)} %get-tuple-element.22.own_ref), channel_id=1, source_target_pairs={{0,1},{2,3},{4,5},{6,7},{8,9},{10,11},{12,13},{14,15},{1,0},{3,2},... | collective-permute-start | bytes 1769480 | tf_op jit(solution)/shard_map/ppermute | solution.py:369
  3.7 13.8 %collective-permute-start.4 = (f32[72,128]{1,0:T(8,128)S(1)}, f32[72,128]{1,0:T(8,128)S(1)}, u32[]{:S(2)}, u32[]{:S(2)}) collective-permute-start(f32[72,128]{1,0:T(8,128)S(1)} %get-tuple-element.23.own_ref), channel_id=1, source_target_pairs={{0,1},{2,3},{4,5},{6,7},{8,9},{10,11},{12,13},{14,15},{1,0},{3,2},... | collective-permute-start | bytes 110600 | tf_op jit(solution)/shard_map/ppermute | solution.py:371
  4.0 22.9 %collective-permute-start.1 = (f32[208,256]{1,0:T(8,128)S(1)}, f32[208,256]{1,0:T(8,128)S(1)}, u32[]{:S(2)}, u32[]{:S(2)}) collective-permute-start(f32[208,256]{1,0:T(8,128)S(1)} %get-tuple-element.21.w_ref), channel_id=1, source_target_pairs={{0,3},{4,7},{8,11},{12,15},{1,2},{5,6},{9,10},{13,14},{3,0},{7,4},... | collective-permute-start | bytes 638984 | tf_op jit(solution)/shard_map/ppermute | solution.py:368
  6.4 26.5 %collective-permute-start.7 = (f32[72,128]{1,0:T(8,128)S(1)}, f32[72,128]{1,0:T(8,128)S(1)}, u32[]{:S(2)}, u32[]{:S(2)}) collective-permute-start(f32[72,128]{1,0:T(8,128)S(1)} %get-tuple-element.23.own_ref), channel_id=1, source_target_pairs={{0,16},{32,48},{64,80},{96,112},{128,144},{160,176},{192,208},{224... | collective-permute-start | bytes 110600 | tf_op jit(solution)/shard_map/ppermute | solution.py:370
  8.0 31.2 %collective-permute-start = (f32[368,256]{1,0:T(8,128)S(1)}, f32[368,256]{1,0:T(8,128)S(1)}, u32[]{:S(2)}, u32[]{:S(2)}) collective-permute-start(f32[368,256]{1,0:T(8,128)S(1)} %get-tuple-element.20.n_ref), channel_id=1, source_target_pairs={{1,2},{3,4},{5,6},{7,8},{9,10},{11,12},{13,14},{2,1},{4,3},{6,5},{... | collective-permute-start | bytes 1130504 | tf_op jit(solution)/shard_map/ppermute | solution.py:367
  17.6 15.4 %copy-start.3 = (f32[286]{0:T(512)S(1)}, f32[286]{0:T(512)}, u32[]{:S(2)}) copy-start(f32[286]{0:T(512)} %relax_ref.1) | copy-start | bytes 3436
  17.6 15.4 %copy-start.4 = (f32[286]{0:T(512)S(1)}, f32[286]{0:T(512)}, u32[]{:S(2)}) copy-start(f32[286]{0:T(512)} %dw_ref.1) | copy-start | bytes 3436
  17.6 4.3 %collective-permute-start.5 = (f32[72,128]{1,0:T(8,128)S(1)}, f32[72,128]{1,0:T(8,128)S(1)}, u32[]{:S(2)}, u32[]{:S(2)}) collective-permute-start(f32[72,128]{1,0:T(8,128)S(1)} %shard_map.123), channel_id=1, source_target_pairs={{17,33},{18,34},{21,37},{22,38},{25,41},{26,42},{29,45},{30,46},{4... | collective-permute-start | bytes 110600 | tf_op jit(solution)/shard_map/ppermute | solution.py:374
  21.9 15.0 %collective-permute-start.6 = (f32[72,128]{1,0:T(8,128)S(1)}, f32[72,128]{1,0:T(8,128)S(1)}, u32[]{:S(2)}, u32[]{:S(2)}) collective-permute-start(f32[72,128]{1,0:T(8,128)S(1)} %collective-permute-done.5.xo_ref), channel_id=1, source_target_pairs={{0,1},{2,3},{4,5},{6,7},{8,9},{10,11},{12,13},{14,15},{1,0},{3,2},... | collective-permute-start | bytes 110600 | tf_op jit(solution)/shard_map/ppermute | solution.py:375
  26.9 15.6 %collective-permute-start.2 = (f32[208,256]{1,0:T(8,128)S(1)}, f32[208,256]{1,0:T(8,128)S(1)}, u32[]{:S(2)}, u32[]{:S(2)}) collective-permute-start(f32[208,256]{1,0:T(8,128)S(1)} %collective-permute-done.1.recv_w_ref), channel_id=1, source_target_pairs={{0,4},{4,8},{8,12},{7,3},{11,7},{15,11},{16,20},{20,24},{24,28},{2... | collective-permute-start | bytes 638984 | tf_op jit(solution)/shard_map/ppermute | solution.py:376
